TPU v7x, 32 devices: a whole 2x2x4 slice. The times are simulated.
32 devices in a mesh: tok: 4 (over y, core), ch: 8 (over z, x).
Axes of the slice: x: 2, y: 2, z: 4, core: 2. Of those that a mesh axis runs over, the one named last changes fastest.
Arguments:
- tokens: bfloat16 [4096, 4096], P('tok', 'ch'), may hold values from -6 to 6
- w_in: bfloat16 [4096, 16384], P('tok', 'ch'), may hold values from -0.09375 to 0.09375
- b_in: float32 [16384], P('ch'), may hold values from -3 to 3
- dw_kernel: float32 [9, 16384], P(None, 'ch'), may hold values from -2 to 2
- dw_bias: float32 [16384], P('ch'), may hold values from -3 to 3
- w_out: bfloat16 [16384, 4096], P('ch', 'tok'), may hold values from -0.0625 to 0.0625
- b_out: float32 [4096], P('ch'), may hold values from -3 to 3
Outputs:
- mixed: bfloat16 [4096, 4096], P('tok', 'ch')
All inputs are finite; a program needn't handle non-finite values.
Results may differ from a plain program's by a relative error of at most 0.0055.
Values may be sent and summed in bfloat16 or wider, within the bound.
No kernel may reach another device: no remote copies, remote signals or barrier semaphores. Data moves between devices by JAX's collectives and lax.ppermute only.
A program may use at most 128 MiB of HBM per device.

v0:
```python
import jax
import jax.numpy as jnp
from jax import lax
from jax.sharding import PartitionSpec as P

IMAGES = 2
GRIDW = 64


def with_halo(array, sides, width):
    for axis, dim in sides:
        size, length = (lax.axis_size(axis), array.shape[dim])
        up = [(i, (i + 1) % size) for i in range(size - 1)]
        down = [(j, i) for i, j in up]
        last = lax.slice_in_dim(array, length - width, length, axis=dim)
        initial = lax.slice_in_dim(array, 0, width, axis=dim)
        before = lax.ppermute(last, axis, up)
        after = lax.ppermute(initial, axis, down)
        array = jnp.concatenate([before, array, after], axis=dim)
    return array


def fetch_rims(grid):
    return with_halo(grid, (("tok", 0),), 1)


def conv_taps(padded, taps, bias, height, width):
    conv = bias + jnp.zeros(
        (height,) + padded.shape[1:2] + (width,) + padded.shape[3:], jnp.float32
    )
    for row_off in range(3):
        for col_off in range(3):
            conv = (
                conv
                + taps[3 * row_off + col_off]
                * padded[row_off : row_off + height, :, col_off : col_off + width, :]
            )
    return conv


def pad_columns(grid):
    return jnp.pad(grid, ((0, 0), (0, 0), (1, 1), (0, 0)))


def local(tokens, w_in, b_in, dw_kernel, dw_bias, w_out, b_out):
    rows = tokens.shape[0]
    hidden = w_in.shape[1]
    w_whole = lax.all_gather(w_in, "tok", axis=0, tiled=True)
    summed = jnp.dot(
        lax.all_gather(tokens, "ch", axis=1, tiled=True),
        w_whole,
        preferred_element_type=jnp.float32,
    )
    pre = (summed + b_in).astype(jnp.bfloat16)
    height = rows // (IMAGES * GRIDW)
    grid = pre.reshape(height, IMAGES, GRIDW, hidden)
    padded = pad_columns(fetch_rims(grid).astype(jnp.float32))
    conv = conv_taps(padded, dw_kernel, dw_bias, height, GRIDW)
    act = jax.nn.gelu(conv, approximate=False).astype(jnp.bfloat16).reshape(rows, hidden)
    w_cols = lax.all_gather(w_out, "tok", axis=1, tiled=True)
    flipped = lax.psum_scatter(
        lax.dot_general(w_cols, act, (((0,), (1,)), ((), ())), preferred_element_type=jnp.float32),
        "ch",
        scatter_dimension=0,
        tiled=True,
    )
    return (flipped.T + b_out).astype(jnp.bfloat16)


def solution(mesh):
    in_specs = (
        P("tok", "ch"),
        P("tok", "ch"),
        P("ch"),
        P(None, "ch"),
        P("ch"),
        P("ch", "tok"),
        P("ch"),
    )
    out_specs = P("tok", "ch")
    return jax.shard_map(local, mesh=mesh, in_specs=in_specs, out_specs=out_specs, check_vma=False)
```

profile of v0, /device:TPU:0, one launch (start us, length us, event | category | flops | bytes accessed | tf_op | source)
XLA Modules:
  0.0 669.0 jit_solution(11230460719229125539)
XLA Ops:
  6.5 0.0 copy-start.3
  6.5 0.0 all-gather.4.cloned.1.call-start
  6.5 0.7 all-gather.4.cloned.1.call-update
  7.3 0.0 all-gather.6.cloned.1.call-start
  7.3 0.7 all-gather.6.cloned.1.call-update
  8.0 0.0 all-gather.8.cloned.1.call-start
  8.1 0.7 all-gather.8.cloned.1.call-update
  8.7 0.0 copy-start
  8.8 0.0 reduce-scatter.2.cloned.1.call-start
  8.8 128.3 %all-gather.4.cloned.1.call-done = bf16[1024,4096]{1,0:T(8,128)(2,1)} async-done(((bf16[1024,512]{1,0:T(8,128)(2,1)}), bf16[1024,4096]{1,0:T(8,128)(2,1)}) %all-gather.4.cloned.1.call-update) | async-done | bytes 8388624 | tf_op jit(solution)/shard_map/all_gather | solution.py:50
  137.1 105.7 %all-gather.6.cloned.1.call-done = bf16[4096,2048]{1,0:T(8,128)(2,1)} async-done(((bf16[1024,2048]{1,0:T(8,128)(2,1)}), bf16[4096,2048]{1,0:T(8,128)(2,1)}) %all-gather.6.cloned.1.call-update) | async-done | bytes 16777232 | tf_op jit(solution)/shard_map/all_gather | solution.py:48
  242.7 0.0 copy-done.3
  242.7 22.7 %add_convert_fusion = bf16[1024,2048]{1,0:T(8,128)(2,1)S(1)} fusion(bf16[1024,4096]{1,0:T(8,128)(2,1)} %all-gather.4.cloned.1.call-done, bf16[4096,2048]{1,0:T(8,128)(2,1)} %all-gather.6.cloned.1.call-done, f32[2048]{0:T(1024)S(1)} %copy-done.3), kind=kOutput, calls=%fused_computation.42 | convolution fusion | flops 17184063488 | bytes 29368320 | tf_op jit(solution)/shard_map/dot_general | solution.py:49
  265.4 0.1 fusion.26
  265.6 0.0 copy-start.1
  265.6 1.3 collective-permute-start.1
  266.9 3.1 collective-permute-start
  269.9 0.0 copy-done
  269.9 0.1 fusion.27
  270.0 0.0 collective-permute-done.1
  270.0 1.9 collective-permute-done
  271.9 0.8 maximum_convert_fusion
  272.7 0.0 copy-done.1
  272.7 27.4 %fusion.17 = bf16[8,2,64,2048]{3,2,1,0:T(8,128)(2,1)} fusion(f32[10,2,64,2048]{3,2,1,0:T(8,128)S(1)} %maximum_convert_fusion, f32[2048]{0:T(1024)S(1)} %bitcast.32, f32[2048]{0:T(1024)S(1)} %bitcast.33, f32[2048]{0:T(1024)S(1)} %bitcast.26, f32[2048]{0:T(1024)S(1)} %bitcast.27, f32[2048]{0:T(1024)S(1)} %bitcast.28, f32[2048]{0:T(1024)S(1)} %bitcast.29, ...), kind=kLoop, calls=%fused_computation.25 | loop fusion | flops 174063616 | bytes 39927808 | tf_op jit(solution)/shard_map/convert_element_type | solution.py:59
  300.2 55.7 %all-gather.8.cloned.1.call-done = bf16[2048,4096]{1,0:T(8,128)(2,1)} async-done(((bf16[2048,1024]{1,0:T(8,128)(2,1)}), bf16[2048,4096]{1,0:T(8,128)(2,1)}) %all-gather.8.cloned.1.call-update) | async-done | bytes 16777232 | tf_op jit(solution)/shard_map/all_gather | solution.py:60
  355.9 23.4 %convolution_bitcast_fusion = f32[4096,1024]{0,1:T(8,128)} fusion(bf16[1024,2048]{1,0:T(8,128)(2,1)} %bitcast.22, bf16[2048,4096]{1,0:T(8,128)(2,1)} %all-gather.8.cloned.1.call-done), kind=kOutput, calls=%fused_computation.7 | convolution fusion | flops 17179869184 | bytes 37748736 | tf_op jit(solution)/shard_map/dot_general | solution.py:62
  379.3 0.0 copy-start.2
  379.3 0.0 reduce-scatter.2.cloned.1.call-update
  379.3 280.3 %reduce-scatter.2.cloned.1.call-done = f32[512,1024]{0,1:T(8,128)} async-done(((f32[4096,1024]{0,1:T(8,128)}), f32[512,1024]{0,1:T(8,128)}) %reduce-scatter.2.cloned.1.call-update) | async-done | bytes 2097168 | tf_op jit(solution)/shard_map/reduce_scatter | solution.py:61
  659.6 0.0 copy-done.2
  659.6 2.8 fusion.25
Async XLA Ops:
  6.5 236.2 %copy-start.3 = (f32[2048]{0:T(1024)S(1)}, f32[2048]{0:T(1024)}, u32[]{:S(2)}) copy-start(f32[2048]{0:T(1024)} %param.9) | copy-start | bytes 24580
  6.5 130.5 %all-gather.4.cloned.1.call-start = ((), (), s32[]{:S(2)}) async-start(), calls=%async_computation.1 | async-start | bytes 9437184 | tf_op jit(solution)/shard_map/all_gather | solution.py:50
  7.3 235.5 %all-gather.6.cloned.1.call-start = ((), (), s32[]{:S(2)}) async-start(), calls=%async_computation.2 | async-start | bytes 20971520 | tf_op jit(solution)/shard_map/all_gather | solution.py:48
  8.0 347.9 %all-gather.8.cloned.1.call-start = ((), (), s32[]{:S(2)}) async-start(), calls=%async_computation.3 | async-start | bytes 20971520 | tf_op jit(solution)/shard_map/all_gather | solution.py:60
  8.7 261.2 %copy-start = (f32[9,2048]{1,0:T(8,128)S(1)}, f32[9,2048]{1,0:T(8,128)}, u32[]{:S(2)}) copy-start(f32[9,2048]{1,0:T(8,128)} %param.10) | copy-start | bytes 221188
  8.8 650.8 %reduce-scatter.2.cloned.1.call-start = ((), (), s32[]{:S(2)}) async-start(), calls=%async_computation.4 | async-start | bytes 18874368 | tf_op jit(solution)/shard_map/reduce_scatter | solution.py:61
  265.6 7.2 %copy-start.1 = (f32[2048]{0:T(1024)S(1)}, f32[2048]{0:T(1024)}, u32[]{:S(2)}) copy-start(f32[2048]{0:T(1024)} %param.11) | copy-start | bytes 24580
  265.6 4.4 collective-permute-start.1
  266.9 5.0 collective-permute-start
  379.3 280.3 %copy-start.2 = (f32[512]{0:T(512)S(1)}, f32[512]{0:T(512)}, u32[]{:S(2)}) copy-start(f32[512]{0:T(512)} %param.13) | copy-start | bytes 6148
Sparse Core Ops, SparseCore 0:
  9.4 127.6 all-gather.3
  138.6 104.0 all-gather.5
  244.3 111.5 all-gather.7
  379.4 280.1 reduce-scatter.1
where the time goes:
time: 669 us
  waiting for transfers between devices  574 us (86%)
  matrix products  46.1 us (7%)
  other arithmetic  31.1 us (5%)
  between operations  13.2 us (2%)
    reduce_scatter x1, waiting for transfers between devices, local(): lax.psum_scatter(lax.dot_general(w_cols, act, (((0,), (1,)), ((), ())), p...  280 us
    all_gather x1, waiting for transfers between devices, local(): lax.all_gather(tokens, 'ch', axis=1, tiled=True)  128 us
    all_gather x1, waiting for transfers between devices, local(): w_whole = lax.all_gather(w_in, 'tok', axis=0, tiled=True)  106 us
    all_gather x1, waiting for transfers between devices, local(): w_cols = lax.all_gather(w_out, 'tok', axis=1, tiled=True)  55.7 us
    convert_element_type x1, other arithmetic, local(): jax.nn.gelu(conv, approximate=False).astype(jnp.bfloat16)  27.4 us
    dot_general x1, matrix products, local(): lax.dot_general(w_cols, act, (((0,), (1,)), ((), ())), preferred_element_...  23.4 us
    dot_general x1, matrix products, local(): jnp.dot(lax.all_gather(tokens, 'ch', axis=1, tiled=True), w_whole, prefer...  22.7 us
  transfers between devices with their start and end apart: 6, of which 5 were waited for; matrix products, arithmetic and copies ran while one was open for 8% of the time, Pallas kernels for 0%

commit v1 on v0

v1 whole, which is shorter than its diff:
```python
import functools

import jax
import jax.numpy as jnp
from jax import lax
from jax.experimental import pallas as pl
from jax.experimental.pallas import tpu as pltpu
from jax.sharding import PartitionSpec as P

IMAGES = 2
GRIDW = 64
BAND = IMAGES * GRIDW
CORES = 2
LANES = 128
HALVES = 2
LAST_SPLITS = 2
CONV_TILE = 512


def blank(*shape):
    return pl.pallas_call(
        lambda ref: None,
        out_shape=jax.ShapeDtypeStruct(shape, jnp.bfloat16),
        out_specs=pl.BlockSpec(memory_space=pl.ANY),
    )()


def conv_kernel(halves, *refs):
    pre_refs = refs[:halves]
    before_ref, after_ref, taps_ref, bias_ref, out_ref, left, right = refs[halves:]
    rows, tile = out_ref.shape
    height = rows // BAND
    per = pl.num_programs(0) // halves

    def run(pre_ref):
        def body(n, _):
            lanes = pl.ds(pl.multiple_of(n // IMAGES * LANES, LANES), LANES)
            first = n % IMAGES * GRIDW
            taps = [taps_ref[i:i + 1, lanes] for i in range(9)]
            bias = bias_ref[:, lanes]
            left[7:8] = jnp.zeros((1, LANES), jnp.float32)
            right[GRIDW:GRIDW + 1] = jnp.zeros((1, LANES), jnp.float32)

            def row(h):
                ref, base = pre_ref, h * BAND
                if h < 0:
                    ref, base = before_ref, 0
                if h >= height:
                    ref, base = after_ref, 0
                at = pl.ds(pl.multiple_of(first + base, GRIDW), GRIDW)
                return at, ref[at, lanes].astype(jnp.float32)

            above, here = row(-1)[1], row(0)[1]
            for h in range(height):
                below = row(h + 1)[1]
                left[8:8 + GRIDW] = above * taps[0] + here * taps[3] + below * taps[6]
                right[0:GRIDW] = above * taps[2] + here * taps[5] + below * taps[8]
                conv = bias + (above * taps[1] + here * taps[4] + below * taps[7])
                conv = conv + left[7:7 + GRIDW] + right[1:1 + GRIDW]
                act = 0.5 * conv * (1.0 + lax.erf(conv * 0.5 ** 0.5))
                at = pl.ds(pl.multiple_of(first + h * BAND, GRIDW), GRIDW)
                out_ref[at, lanes] = act.astype(out_ref.dtype)
                above, here = here, below
            return 0

        lax.fori_loop(0, IMAGES * (tile // LANES), body, 0)

    for f in range(halves):
        pl.when(pl.program_id(0) // per == f)(functools.partial(run, pre_refs[f]))


def convolve(pres, before, after, taps, bias):
    rows, part = pres[0].shape
    halves = len(pres)
    tile = min(CONV_TILE, part)
    per = part // tile

    def pre_map(f):
        return lambda i: (0, jnp.clip(i - f * per, 0, per - 1))

    def wide(n):
        return pl.BlockSpec((n, tile), lambda i: (0, i))

    return pl.pallas_call(
        functools.partial(conv_kernel, halves),
        grid=(halves * per,),
        in_specs=[pl.BlockSpec((rows, tile), pre_map(f)) for f in range(halves)]
        + [wide(BAND), wide(BAND), wide(9), wide(1)],
        out_specs=wide(rows),
        out_shape=jax.ShapeDtypeStruct((rows, halves * part), jnp.bfloat16),
        scratch_shapes=[pltpu.VMEM((GRIDW + 16, LANES), jnp.float32)] * 2,
        compiler_params=pltpu.CompilerParams(vmem_limit_bytes=24 << 20),
        cost_estimate=pl.CostEstimate(flops=60 * rows * halves * part, bytes_accessed=4 * rows * halves * part, transcendentals=0),
    )(*pres, before, after, taps, bias[None])


def local(tokens, w_in, b_in, dw_kernel, dw_bias, w_out, b_out):
    nt, nc = lax.axis_size("tok"), lax.axis_size("ch")
    nz, nx, ny = nt, nc // nt, nt // CORES
    t, c = lax.axis_index("tok"), lax.axis_index("ch")
    z, x = c // nx, c % nx
    y, core = t // CORES, t % CORES
    rows, width = tokens.shape
    depth, hidden = w_in.shape
    part = hidden // HALVES

    def zshift(k):
        return [(i, (i + k * nx) % nc) for i in range(nc)]

    def xshift(k):
        return [(i, i // nx * nx + (i + k) % nx) for i in range(nc)]

    def yshift(k):
        return [(i, (i + CORES * k) % nt) for i in range(nt)]

    swap = [(i, i ^ 1) for i in range(nt)]

    def owner(k, other):
        return (y + ny - k) % ny * CORES + (1 - core if other else core)

    held = tokens
    span = nx * width
    early = (nz - 1) * span
    whole = blank(rows, early)
    last = blank(rows, span)
    for s in range(nz):
        if s:
            held = lax.ppermute(held, "ch", zshift(1))
        for k in range(nx):
            block = lax.ppermute(held, "ch", xshift(k)) if k else held
            start = (x + nx - k) % nx * width
            if s < nz - 1:
                whole = lax.dynamic_update_slice_in_dim(whole, block, s * span + start, 1)
            else:
                last = lax.dynamic_update_slice_in_dim(last, block, start, 1)

    partner = lax.ppermute(w_in, "tok", swap)
    pres = []
    for f in range(HALVES):
        cut = slice(f * part, (f + 1) * part)
        stack = blank(nz * depth, part)
        for k in range(ny):
            mine = lax.ppermute(w_in[:, cut], "tok", yshift(k)) if k else w_in[:, cut]
            pair = lax.ppermute(mine, "tok", swap) if k else partner[:, cut]
            for other, block in ((0, mine), (1, pair)):
                stack = lax.dynamic_update_slice_in_dim(stack, block, (z + nz - owner(k, other)) % nz * depth, 0)
        total = jnp.dot(whole, stack[:early], preferred_element_type=jnp.float32)
        total = total + jnp.dot(last, stack[early:], preferred_element_type=jnp.float32)
        pres.append((total + b_in[cut]).astype(jnp.bfloat16))

    up = [(i, i + 1) for i in range(nt - 1)]
    down = [(i + 1, i) for i in range(nt - 1)]
    before = lax.ppermute(jnp.concatenate([p[-BAND:] for p in pres], axis=1), "tok", up)
    after = lax.ppermute(jnp.concatenate([p[:BAND] for p in pres], axis=1), "tok", down)
    act = convolve(pres, before, after, dw_kernel, dw_bias)

    pieces = max(1, width // LANES)
    cols = width // pieces
    outs = []
    for q in range(pieces):
        piece = jnp.concatenate(
            [lax.dynamic_slice_in_dim(w_out, (x + k) % nx * width + q * cols, cols, 1) for k in range(nx)], axis=1
        )
        blocks = []
        for k in range(ny):
            mine = lax.ppermute(piece, "tok", yshift(k)) if k else piece
            blocks += [mine, lax.ppermute(mine, "tok", swap)]
        dots = [jnp.dot(act, b, preferred_element_type=jnp.float32) for b in blocks]
        base = jnp.concatenate([d[:, :cols] for d in dots], axis=1)
        splits = LAST_SPLITS if q == pieces - 1 else 1
        step = rows // splits
        bands = []
        for h in range(splits):
            cut = slice(h * step, (h + 1) * step)
            total = base[cut]
            if h:
                total, _ = lax.optimization_barrier((total, done))
            for k in range(1, nx):
                share = jnp.concatenate([d[cut, k * cols:(k + 1) * cols].astype(jnp.bfloat16) for d in dots], axis=1)
                other = lax.ppermute(share, "ch", xshift(k))
                total = total + other.astype(jnp.float32)

            def term(s):
                goal = (z + nz - s) % nz
                place = (y + ny - goal // CORES) % ny * CORES + (goal + core) % CORES
                return lax.dynamic_slice_in_dim(total, place * cols, cols, 1)

            done = term(0)
            for s in range(1, nz):
                done = done + lax.ppermute(term(s).astype(jnp.bfloat16), "ch", zshift(nz - s)).astype(jnp.float32)
            bands.append(done)
        outs.append(jnp.concatenate(bands, axis=0))
    return (jnp.concatenate(outs, axis=1) + b_out).astype(jnp.bfloat16)


def solution(mesh):
    in_specs = (
        P("tok", "ch"),
        P("tok", "ch"),
        P("ch"),
        P(None, "ch"),
        P("ch"),
        P("ch", "tok"),
        P("ch"),
    )
    return jax.shard_map(local, mesh=mesh, in_specs=in_specs, out_specs=P("tok", "ch"), check_vma=False)
```

time: 669 us -> 376 us (0.56)
  waiting for transfers between devices: 574 us -> 183 us
  starting transfers between devices: 4.47 us -> 84.1 us
  local copies, waits for them, and re-layouts: 0.17 us -> 39.3 us
  other arithmetic: 31.1 us -> 8.4 us
  between operations: 13.2 us -> 1.47 us
  Pallas kernels: 0 us -> 8.99 us
    all_gather x3 -> x0, waiting for transfers between devices: 290 us -> none  [the longest x1 128 us: local(): lax.all_gather(tokens, 'ch', axis=1, tiled=True)]
    reduce_scatter x1 -> x0, waiting for transfers between devices: 280 us -> none  [local(): lax.psum_scatter(lax.dot_general(w_cols, act, (((0,), (1,)), ((), ())), p...]
    ppermute x2 -> x46, waiting for transfers between devices: 1.88 us -> 183 us  [the longest x5 46.5 us: local(): other = lax.ppermute(share, 'ch', xshift(k))]
    ppermute x2 -> x46, starting transfers between devices: 4.36 us -> 84.1 us  [the longest x15 38.1 us: local(): lax.ppermute(term(s).astype(jnp.bfloat16), 'ch', zshift(nz - s))]
    convert_element_type x3 -> x1, other arithmetic: 31.1 us -> 0.18 us  [local(): return (jnp.concatenate(outs, axis=1) + b_out).astype(jnp.bfloat16)]
    dynamic_update_slice x0 -> x13, local copies, waits for them, and re-layouts: none -> 26.3 us  [the longest x6 13.3 us: local(): whole = lax.dynamic_update_slice_in_dim(whole, block, s * span + start, 1)]
    pallas_call x0 -> x5, Pallas kernels: none -> 8.99 us  [the longest x1 8.98 us: convolve(): pl.pallas_call(functools.partial(conv_kernel, halves), grid=(halves * per...]
    dot_general x2 -> x20, matrix products: 46.1 us -> 46.7 us  [the longest x16 24.5 us: local(): dots = [jnp.dot(act, b, preferred_element_type=jnp.float32) for b in blocks]]
  transfers between devices with their start and end apart: 6 -> 46, of which waited for: 5 -> 17; matrix products, arithmetic and copies ran while one was open for 8% -> 25% of each run, Pallas kernels for 0% -> 2%
where the time goes in v1:
time: 376 us; the launch traced here: 372 us
  waiting for transfers between devices  183 us (49%)
  starting transfers between devices  84.1 us (22%)
  matrix products  46.7 us (12%)
  local copies, waits for them, and re-layouts  39.3 us (10%)
  Pallas kernels  8.99 us (2%)
  other arithmetic  8.4 us (2%)
    ppermute x5, waiting for transfers between devices, local(): other = lax.ppermute(share, 'ch', xshift(k))  46.5 us
    ppermute x15, waiting for transfers between devices, local(): lax.ppermute(term(s).astype(jnp.bfloat16), 'ch', zshift(nz - s))  42.3 us
    ppermute x15, starting transfers between devices, local(): lax.ppermute(term(s).astype(jnp.bfloat16), 'ch', zshift(nz - s))  38.1 us
    ppermute x3, waiting for transfers between devices, local(): held = lax.ppermute(held, 'ch', zshift(1))  31.3 us
    ppermute x4, waiting for transfers between devices, local(): mine = lax.ppermute(piece, 'tok', yshift(k)) if k else piece  28.3 us
    dot_general x16, matrix products, local(): dots = [jnp.dot(act, b, preferred_element_type=jnp.float32) for b in blocks]  24.5 us
    ppermute x2, waiting for transfers between devices, local(): mine = lax.ppermute(w_in[:, cut], 'tok', yshift(k)) if k else w_in[:, cut]  24 us
    ppermute x8, starting transfers between devices, local(): blocks += [mine, lax.ppermute(mine, 'tok', swap)]  21.1 us
  transfers between devices with their start and end apart: 46, of which 17 were waited for; matrix products, arithmetic and copies ran while one was open for 25% of the time, Pallas kernels for 2%

profile of v1, /device:TPU:0, one launch (start us, length us, event | category | flops | bytes accessed | tf_op | source)
XLA Modules:
  0.0 371.8 jit_solution(8462658978457391327)
XLA Ops:
  0.5 5.5 %fusion.17 = (bf16[1024,1024]{1,0:T(8,128)(2,1)}, bf16[4096,1024]{1,0:T(8,128)(2,1)}, bf16[4096,1024]{1,0:T(8,128)(2,1)}, bf16[1024,1024]{1,0:T(8,128)(2,1)S(1)}) fusion(bf16[1024,2048]{1,0:T(8,128)(2,1)} %param.8, bf16[4096,1024]{1,0:T(8,128)(2,1)} %shard_map.74, s32[]{:T(128)S(6)} %select_n.376, bf16[4096,1024]{1,0:T(8,128)(2,1)} %shard_map.76), kind=kLoop, calls=%fused_computation.89 | loop fusion | bytes 12582916 | tf_op jit(solution)/shard_map/slice | solution.py:143
  11.5 24.2 %collective-permute-done.1 = bf16[1024,512]{1,0:T(8,128)(2,1)} collective-permute-done((bf16[1024,512]{1,0:T(8,128)(2,1)S(1)}, bf16[1024,512]{1,0:T(8,128)(2,1)}, u32[]{:S(2)}, u32[]{:S(2)}) %collective-permute-start.1) | collective-permute-done | bytes 1048608 | tf_op jit(solution)/shard_map/ppermute | solution.py:128
  38.7 3.9 %constant_dynamic-slice_fusion.7 = (bf16[2048,128]{1,0:T(8,128)(2,1)S(1)}, bf16[2048,128]{1,0:T(8,128)(2,1)}, bf16[2048,128]{1,0:T(8,128)(2,1)}, bf16[2048,128]{...) fusion(bf16[2048,1024]{1,0:T(8,128)(2,1)} %param.12, ...), kind=kLoop, calls=%fused_computation.70 | loop fusion | bytes 8388640 | tf_op jit(solution)/shard_map/dynamic_slice | solution.py:162
  42.6 12.6 %collective-permute-done.10 = bf16[1024,1024]{1,0:T(8,128)(2,1)} collective-permute-done((bf16[1024,1024]{1,0:T(8,128)(2,1)}, bf16[1024,1024]{1,0:T(8,128)(2,1)}, u32[]{:S(2)}, u32[]{:S(2)}) %collective-permute-start.10) | collective-permute-done | bytes 2097184 | tf_op jit(solution)/shard_map/ppermute | solution.py:143
  55.3 7.1 %collective-permute-done.3 = bf16[1024,512]{1,0:T(8,128)(2,1)} collective-permute-done((bf16[1024,512]{1,0:T(8,128)(2,1)}, bf16[1024,512]{1,0:T(8,128)(2,1)}, u32[]{:S(2)}, u32[]{:S(2)}) %collective-permute-start.3) | collective-permute-done | bytes 1048608 | tf_op jit(solution)/shard_map/ppermute | solution.py:128
  70.9 2.5 constant_dynamic-update-slice_fusion.10
  76.0 10.3 %collective-permute-done.4 = bf16[1024,512]{1,0:T(8,128)(2,1)} collective-permute-done((bf16[1024,512]{1,0:T(8,128)(2,1)}, bf16[1024,512]{1,0:T(8,128)(2,1)}, u32[]{:S(2)}, u32[]{:S(2)}) %collective-permute-start.4) | collective-permute-done | bytes 1048608 | tf_op jit(solution)/shard_map/ppermute | solution.py:130
  88.6 11.4 %collective-permute-done.6 = bf16[1024,1024]{1,0:T(8,128)(2,1)} collective-permute-done((bf16[1024,1024]{1,0:T(8,128)(2,1)S(1)}, bf16[1024,1024]{1,0:T(8,128)(2,1)}, u32[]{:S(2)}, u32[]{:S(2)}) %collective-permute-start.6) | collective-permute-done | bytes 2097184 | tf_op jit(solution)/shard_map/ppermute | solution.py:143
  103.5 4.0 %slice_dynamic-update-slice_fusion = (bf16[4096,1024]{1,0:T(8,128)(2,1)}, bf16[4096,1024]{1,0:T(8,128)(2,1)S(1)}) fusion(bf16[4096,1024]{1,0:T(8,128)(2,1)} %get-tuple-element.17, s32[]{:T(128)S(6)} %select_n.378, bf16[1024,2048]{1,0:T(8,128)(2,1)} %collective-permute-done.5, bf16[4096,1024]{1,0:T(8,128)(2,1)S(1)} %bitcast.35), kind=kLoop, calls=%fused_computation.8 | loop fusion | bytes 8388612 | tf_op jit(solution)/shard_map/dynamic_update_slice | solution.py:146
  107.5 3.2 constant_dynamic-update-slice_fusion.1
  112.8 3.1 constant_dynamic-update-slice_fusion
  115.9 9.2 %fusion = f32[1024,1024]{1,0:T(8,128)S(1)} fusion(bf16[1024,3072]{1,0:T(8,128)(2,1)S(1)} %bitcast.37, bf16[4096,1024]{1,0:T(8,128)(2,1)} %constant_dynamic-update-slice_fusion), kind=kOutput, calls=%fused_computation | convolution fusion | flops 6442450944 | bytes 16777216 | tf_op jit(solution)/shard_map/dot_general | solution.py:147
  125.4 6.7 %fusion.2 = f32[1024,1024]{1,0:T(8,128)S(1)} fusion(bf16[1024,3072]{1,0:T(8,128)(2,1)S(1)} %bitcast.37, bf16[4096,1024]{1,0:T(8,128)(2,1)S(1)} %constant_dynamic-update-slice_fusion.5), kind=kOutput, calls=%fused_computation.2 | convolution fusion | flops 6442450944 | bytes 16777216 | tf_op jit(solution)/shard_map/dot_general | solution.py:147
  132.3 4.0 %add_convert_fusion.refs_1_ = bf16[1024,1024]{1,0:T(8,128)(2,1)S(1)} fusion(f32[1024,1024]{1,0:T(8,128)S(1)} %fusion, f32[1024]{0:T(1024)S(1)} %get-tuple-element.50, bf16[1024,1024]{1,0:T(8,128)(2,1)S(1)} %constant_dynamic-update-slice_fusion.3, bf16[4096,1024]{1,0:T(8,128)(2,1)} %constant_dynamic-update-slice_fusion), kind=kOutput, calls=%fused_computation.4 | convolution fusion | flops 2150629376 | bytes 10489856 | tf_op jit(solution)/shard_map/dot_general | solution.py:148
  141.8 3.1 collective-permute-start.12
  151.1 5.4 %collective-permute-start.16 = (bf16[2048,256]{1,0:T(8,128)(2,1)}, bf16[2048,256]{1,0:T(8,128)(2,1)S(1)}, u32[]{:S(2)}, u32[]{:S(2)}) collective-permute-start(bf16[2048,256]{1,0:T(8,128)(2,1)} %collective-permute-done.15), channel_id=1, source_target_pairs={{0,8},{8,0},{16,24},{24,16},{1,9},{9,1},{17,25},{25,17},{2,10},{10... | collective-permute-start | bytes 3145736 | tf_op jit(solution)/shard_map/ppermute | solution.py:167
  156.6 9.0 %shard_map.77 = bf16[1024,2048]{1,0:T(8,128)(2,1)S(1)} custom-call(bf16[1024,1024]{1,0:T(8,128)(2,1)S(1)} %copy-done.1, bf16[1024,1024]{1,0:T(8,128)(2,1)S(1)} %add_convert_fusion.refs_1_, bf16[128,2048]{1,0:T(8,128)(2,1)S(1)} %collective-permute-done.12.refs_2_, bf16[128,2048]{1,0:T(8,128)(2,1)S(1)} %collective-permute-done.13.refs_3_, ...), custom_call_target="tpu_custom_call" | custom-call | flops 125829120 | bytes 8388608 | tf_op jit(solution)/shard_map/pallas_call | solution.py:84
  176.5 6.8 %collective-permute-start.23 = (bf16[2048,256]{1,0:T(8,128)(2,1)}, bf16[2048,256]{1,0:T(8,128)(2,1)S(1)}, u32[]{:S(2)}, u32[]{:S(2)}) collective-permute-start(bf16[2048,256]{1,0:T(8,128)(2,1)} %collective-permute-done.22), channel_id=1, source_target_pairs={{0,8},{8,0},{16,24},{24,16},{1,9},{9,1},{17,25},{25,17},{2,10},{10... | collective-permute-start | bytes 3145736 | tf_op jit(solution)/shard_map/ppermute | solution.py:167
  186.1 10.1 %collective-permute-done.29 = bf16[2048,256]{1,0:T(8,128)(2,1)S(1)} collective-permute-done((bf16[2048,256]{1,0:T(8,128)(2,1)S(1)}, bf16[2048,256]{1,0:T(8,128)(2,1)S(1)}, u32[]{:S(2)}, u32[]{:S(2)}) %collective-permute-start.29) | collective-permute-done | bytes 1048608 | tf_op jit(solution)/shard_map/ppermute | solution.py:166
  196.3 4.6 %collective-permute-start.30 = (bf16[2048,256]{1,0:T(8,128)(2,1)S(1)}, bf16[2048,256]{1,0:T(8,128)(2,1)S(1)}, u32[]{:S(2)}, u32[]{:S(2)}) collective-permute-start(bf16[2048,256]{1,0:T(8,128)(2,1)S(1)} %collective-permute-done.29), channel_id=1, source_target_pairs={{0,8},{8,0},{16,24},{24,16},{1,9},{9,1},{17,25},{25,17},{2,10},{10... | collective-permute-start | bytes 3145736 | tf_op jit(solution)/shard_map/ppermute | solution.py:167
  200.9 17.3 %collective-permute-done.36 = bf16[2048,256]{1,0:T(8,128)(2,1)S(1)} collective-permute-done((bf16[2048,256]{1,0:T(8,128)(2,1)S(1)}, bf16[2048,256]{1,0:T(8,128)(2,1)S(1)}, u32[]{:S(2)}, u32[]{:S(2)}) %collective-permute-start.36) | collective-permute-done | bytes 1048608 | tf_op jit(solution)/shard_map/ppermute | solution.py:166
  238.4 32.1 %collective-permute-done.38 = bf16[512,512]{0,1:T(8,128)(2,1)S(1)} collective-permute-done((bf16[512,512]{0,1:T(8,128)(2,1)S(1)}, bf16[512,512]{0,1:T(8,128)(2,1)S(1)}, u32[]{:S(2)}, u32[]{:S(2)}) %collective-permute-start.38) | collective-permute-done | bytes 524320 | tf_op jit(solution)/shard_map/ppermute | solution.py:180
  270.9 3.7 collective-permute-start.39
  275.9 2.6 collective-permute-done.39
  279.0 6.4 %collective-permute-done.40 = bf16[512,128]{0,1:T(8,128)(2,1)S(1)} collective-permute-done((bf16[512,128]{0,1:T(8,128)(2,1)S(1)}, bf16[512,128]{0,1:T(8,128)(2,1)S(1)}, u32[]{:S(2)}, u32[]{:S(2)}) %collective-permute-start.40) | collective-permute-done | bytes 131104 | tf_op jit(solution)/shard_map/ppermute | solution.py:190
  292.1 7.4 %collective-permute-done.44 = bf16[512,128]{0,1:T(8,128)(2,1)S(1)} collective-permute-done((bf16[512,128]{0,1:T(8,128)(2,1)S(1)}, bf16[512,128]{0,1:T(8,128)(2,1)S(1)}, u32[]{:S(2)}, u32[]{:S(2)}) %collective-permute-start.44) | collective-permute-done | bytes 131104 | tf_op jit(solution)/shard_map/ppermute | solution.py:190
  305.1 4.3 %collective-permute-start.25 = (bf16[1024,128]{0,1:T(8,128)(2,1)S(1)}, bf16[1024,128]{0,1:T(8,128)(2,1)S(1)}, u32[]{:S(2)}, u32[]{:S(2)}) collective-permute-start(bf16[1024,128]{0,1:T(8,128)(2,1)S(1)} %get-tuple-element.24), channel_id=1, source_target_pairs={{0,6},{1,7},{2,0},{3,1},{4,2},{5,3},{6,4},{7,5},{8,14},{9,15},{10,... | collective-permute-start | bytes 786440 | tf_op jit(solution)/shard_map/ppermute | solution.py:190
  309.5 13.5 %collective-permute-done.31 = bf16[1024,512]{0,1:T(8,128)(2,1)S(1)} collective-permute-done((bf16[1024,512]{0,1:T(8,128)(2,1)S(1)}, bf16[1024,512]{0,1:T(8,128)(2,1)S(1)}, u32[]{:S(2)}, u32[]{:S(2)}) %collective-permute-start.31) | collective-permute-done | bytes 1048608 | tf_op jit(solution)/shard_map/ppermute | solution.py:180
  324.6 3.6 collective-permute-start.27
  328.6 14.0 %collective-permute-start.33 = (bf16[1024,128]{0,1:T(8,128)(2,1)S(1)}, bf16[1024,128]{0,1:T(8,128)(2,1)S(1)}, u32[]{:S(2)}, u32[]{:S(2)}) collective-permute-start(bf16[1024,128]{0,1:T(8,128)(2,1)S(1)} %get-tuple-element.29), channel_id=1, source_target_pairs={{0,4},{1,5},{2,6},{3,7},{4,0},{5,1},{6,2},{7,3},{8,12},{9,13},{10,... | collective-permute-start | bytes 786440 | tf_op jit(solution)/shard_map/ppermute | solution.py:190
  345.0 14.3 %collective-permute-done.26 = bf16[1024,128]{0,1:T(8,128)(2,1)S(1)} collective-permute-done((bf16[1024,128]{0,1:T(8,128)(2,1)S(1)}, bf16[1024,128]{0,1:T(8,128)(2,1)S(1)}, u32[]{:S(2)}, u32[]{:S(2)}) %collective-permute-start.26) | collective-permute-done | bytes 262176 | tf_op jit(solution)/shard_map/ppermute | solution.py:190
  359.5 10.4 %collective-permute-done.33 = bf16[1024,128]{0,1:T(8,128)(2,1)S(1)} collective-permute-done((bf16[1024,128]{0,1:T(8,128)(2,1)S(1)}, bf16[1024,128]{0,1:T(8,128)(2,1)S(1)}, u32[]{:S(2)}, u32[]{:S(2)}) %collective-permute-start.33) | collective-permute-done | bytes 262176 | tf_op jit(solution)/shard_map/ppermute | solution.py:190
  (253 shorter events, 94.0 us)
Async XLA Ops:
  0.0 101.9 %collective-permute-start.5 = (bf16[1024,2048]{1,0:T(8,128)(2,1)}, bf16[1024,2048]{1,0:T(8,128)(2,1)}, u32[]{:S(2)}, u32[]{:S(2)}) collective-permute-start(bf16[1024,2048]{1,0:T(8,128)(2,1)} %param.8), channel_id=1, source_target_pairs={{0,8},{8,0},{16,24},{24,16},{1,9},{9,1},{17,25},{25,17},{2,10},{10... | collective-permute-start | bytes 12582920 | tf_op jit(solution)/shard_map/ppermute | solution.py:137
  6.0 49.3 %collective-permute-start.10 = (bf16[1024,1024]{1,0:T(8,128)(2,1)}, bf16[1024,1024]{1,0:T(8,128)(2,1)}, u32[]{:S(2)}, u32[]{:S(2)}) collective-permute-start(bf16[1024,1024]{1,0:T(8,128)(2,1)} %get-tuple-element.15), channel_id=1, source_target_pairs={{0,16},{8,24},{16,0},{24,8},{1,17},{9,25},{17,1},{25,9},{2,18},{10... | collective-permute-start | bytes 6291464 | tf_op jit(solution)/shard_map/ppermute | solution.py:143
  8.5 27.3 %collective-permute-start.1 = (bf16[1024,512]{1,0:T(8,128)(2,1)S(1)}, bf16[1024,512]{1,0:T(8,128)(2,1)}, u32[]{:S(2)}, u32[]{:S(2)}) collective-permute-start(bf16[1024,512]{1,0:T(8,128)(2,1)S(1)} %copy-done.29), channel_id=1, source_target_pairs={{0,2},{1,3},{2,4},{3,5},{4,6},{5,7},{6,0},{7,1},{8,10},{9,11},{10,... | collective-permute-start | bytes 3145736 | tf_op jit(solution)/shard_map/ppermute | solution.py:128
  10.0 27.2 %collective-permute-start = (bf16[1024,512]{1,0:T(8,128)(2,1)S(1)}, bf16[1024,512]{1,0:T(8,128)(2,1)S(1)}, u32[]{:S(2)}, u32[]{:S(2)}) collective-permute-start(bf16[1024,512]{1,0:T(8,128)(2,1)S(1)} %copy-done.29), channel_id=1, source_target_pairs={{0,1},{1,0},{2,3},{3,2},{4,5},{5,4},{6,7},{7,6},{8,9},{9,8},{10,11... | collective-permute-start | bytes 3145736 | tf_op jit(solution)/shard_map/ppermute | solution.py:130
  35.7 26.6 %collective-permute-start.3 = (bf16[1024,512]{1,0:T(8,128)(2,1)}, bf16[1024,512]{1,0:T(8,128)(2,1)}, u32[]{:S(2)}, u32[]{:S(2)}) collective-permute-start(bf16[1024,512]{1,0:T(8,128)(2,1)} %collective-permute-done.1), channel_id=1, source_target_pairs={{0,2},{1,3},{2,4},{3,5},{4,6},{5,7},{6,0},{7,1},{8,10},{9,11},{10,... | collective-permute-start | bytes 3145736 | tf_op jit(solution)/shard_map/ppermute | solution.py:128
  35.7 28.1 %collective-permute-start.2 = (bf16[1024,512]{1,0:T(8,128)(2,1)}, bf16[1024,512]{1,0:T(8,128)(2,1)}, u32[]{:S(2)}, u32[]{:S(2)}) collective-permute-start(bf16[1024,512]{1,0:T(8,128)(2,1)} %collective-permute-done.1), channel_id=1, source_target_pairs={{0,1},{1,0},{2,3},{3,2},{4,5},{5,4},{6,7},{7,6},{8,9},{9,8},{10,11... | collective-permute-start | bytes 3145736 | tf_op jit(solution)/shard_map/ppermute | solution.py:130
  38.2 61.8 %collective-permute-start.6 = (bf16[1024,1024]{1,0:T(8,128)(2,1)S(1)}, bf16[1024,1024]{1,0:T(8,128)(2,1)}, u32[]{:S(2)}, u32[]{:S(2)}) collective-permute-start(bf16[1024,1024]{1,0:T(8,128)(2,1)S(1)} %get-tuple-element.18), channel_id=1, source_target_pairs={{0,16},{8,24},{16,0},{24,8},{1,17},{9,25},{17,1},{25,9},{2,18},{10... | collective-permute-start | bytes 6291464 | tf_op jit(solution)/shard_map/ppermute | solution.py:143
  55.3 57.5 %collective-permute-start.11 = (bf16[1024,1024]{1,0:T(8,128)(2,1)}, bf16[1024,1024]{1,0:T(8,128)(2,1)}, u32[]{:S(2)}, u32[]{:S(2)}) collective-permute-start(bf16[1024,1024]{1,0:T(8,128)(2,1)} %collective-permute-done.10), channel_id=1, source_target_pairs={{0,8},{8,0},{16,24},{24,16},{1,9},{9,1},{17,25},{25,17},{2,10},{10... | collective-permute-start | bytes 6291464 | tf_op jit(solution)/shard_map/ppermute | solution.py:144
  63.8 37.9 %collective-permute-start.8 = (bf16[1024,512]{1,0:T(8,128)(2,1)}, bf16[1024,512]{1,0:T(8,128)(2,1)S(1)}, u32[]{:S(2)}, u32[]{:S(2)}) collective-permute-start(bf16[1024,512]{1,0:T(8,128)(2,1)} %collective-permute-done.3), channel_id=1, source_target_pairs={{0,2},{1,3},{2,4},{3,5},{4,6},{5,7},{6,0},{7,1},{8,10},{9,11},{10,... | collective-permute-start | bytes 3145736 | tf_op jit(solution)/shard_map/ppermute | solution.py:128
  86.3 81.8 %collective-permute-start.14 = (bf16[2048,256]{1,0:T(8,128)(2,1)}, bf16[2048,256]{1,0:T(8,128)(2,1)}, u32[]{:S(2)}, u32[]{:S(2)}) collective-permute-start(bf16[2048,256]{1,0:T(8,128)(2,1)} %pad_maximum_fusion.1), channel_id=1, source_target_pairs={{0,8},{8,0},{16,24},{24,16},{1,9},{9,1},{17,25},{25,17},{2,10},{10... | collective-permute-start | bytes 3145736 | tf_op jit(solution)/shard_map/ppermute | solution.py:167
  100.0 48.9 %collective-permute-start.15 = (bf16[2048,256]{1,0:T(8,128)(2,1)}, bf16[2048,256]{1,0:T(8,128)(2,1)}, u32[]{:S(2)}, u32[]{:S(2)}) collective-permute-start(bf16[2048,256]{1,0:T(8,128)(2,1)} %pad_maximum_fusion.1), channel_id=1, source_target_pairs={{0,16},{8,24},{16,0},{24,8},{1,17},{9,25},{17,1},{25,9},{2,18},{10... | collective-permute-start | bytes 3145736 | tf_op jit(solution)/shard_map/ppermute | solution.py:166
  101.9 30.1 %collective-permute-start.9 = (bf16[1024,512]{1,0:T(8,128)(2,1)S(1)}, bf16[1024,512]{1,0:T(8,128)(2,1)S(1)}, u32[]{:S(2)}, u32[]{:S(2)}) collective-permute-start(bf16[1024,512]{1,0:T(8,128)(2,1)S(1)} %collective-permute-done.8), channel_id=1, source_target_pairs={{0,1},{1,0},{2,3},{3,2},{4,5},{5,4},{6,7},{7,6},{8,9},{9,8},{10,11... | collective-permute-start | bytes 3145736 | tf_op jit(solution)/shard_map/ppermute | solution.py:130
  146.0 27.9 %collective-permute-start.22 = (bf16[2048,256]{1,0:T(8,128)(2,1)}, bf16[2048,256]{1,0:T(8,128)(2,1)}, u32[]{:S(2)}, u32[]{:S(2)}) collective-permute-start(bf16[2048,256]{1,0:T(8,128)(2,1)} %pad_maximum_fusion.3), channel_id=1, source_target_pairs={{0,16},{8,24},{16,0},{24,8},{1,17},{9,25},{17,1},{25,9},{2,18},{10... | collective-permute-start | bytes 3145736 | tf_op jit(solution)/shard_map/ppermute | solution.py:166
  148.9 37.0 %collective-permute-start.21 = (bf16[2048,256]{1,0:T(8,128)(2,1)}, bf16[2048,256]{1,0:T(8,128)(2,1)S(1)}, u32[]{:S(2)}, u32[]{:S(2)}) collective-permute-start(bf16[2048,256]{1,0:T(8,128)(2,1)} %pad_maximum_fusion.3), channel_id=1, source_target_pairs={{0,8},{8,0},{16,24},{24,16},{1,9},{9,1},{17,25},{25,17},{2,10},{10... | collective-permute-start | bytes 3145736 | tf_op jit(solution)/shard_map/ppermute | solution.py:167
  149.1 86.5 %collective-permute-start.28 = (bf16[2048,256]{1,0:T(8,128)(2,1)S(1)}, bf16[2048,256]{1,0:T(8,128)(2,1)S(1)}, u32[]{:S(2)}, u32[]{:S(2)}) collective-permute-start(bf16[2048,256]{1,0:T(8,128)(2,1)S(1)} %pad_maximum_fusion.5), channel_id=1, source_target_pairs={{0,8},{8,0},{16,24},{24,16},{1,9},{9,1},{17,25},{25,17},{2,10},{10... | collective-permute-start | bytes 3145736 | tf_op jit(solution)/shard_map/ppermute | solution.py:167
  168.1 28.1 %collective-permute-start.29 = (bf16[2048,256]{1,0:T(8,128)(2,1)S(1)}, bf16[2048,256]{1,0:T(8,128)(2,1)S(1)}, u32[]{:S(2)}, u32[]{:S(2)}) collective-permute-start(bf16[2048,256]{1,0:T(8,128)(2,1)S(1)} %pad_maximum_fusion.5), channel_id=1, source_target_pairs={{0,16},{8,24},{16,0},{24,8},{1,17},{9,25},{17,1},{25,9},{2,18},{10... | collective-permute-start | bytes 3145736 | tf_op jit(solution)/shard_map/ppermute | solution.py:166
  173.9 44.3 %collective-permute-start.36 = (bf16[2048,256]{1,0:T(8,128)(2,1)S(1)}, bf16[2048,256]{1,0:T(8,128)(2,1)S(1)}, u32[]{:S(2)}, u32[]{:S(2)}) collective-permute-start(bf16[2048,256]{1,0:T(8,128)(2,1)S(1)} %pad_maximum_fusion.7), channel_id=1, source_target_pairs={{0,16},{8,24},{16,0},{24,8},{1,17},{9,25},{17,1},{25,9},{2,18},{10... | collective-permute-start | bytes 3145736 | tf_op jit(solution)/shard_map/ppermute | solution.py:166
  176.5 46.5 %collective-permute-start.23 = (bf16[2048,256]{1,0:T(8,128)(2,1)}, bf16[2048,256]{1,0:T(8,128)(2,1)S(1)}, u32[]{:S(2)}, u32[]{:S(2)}) collective-permute-start(bf16[2048,256]{1,0:T(8,128)(2,1)} %collective-permute-done.22), channel_id=1, source_target_pairs={{0,8},{8,0},{16,24},{24,16},{1,9},{9,1},{17,25},{25,17},{2,10},{10... | collective-permute-start | bytes 3145736 | tf_op jit(solution)/shard_map/ppermute | solution.py:167
  185.9 40.6 %collective-permute-start.35 = (bf16[2048,256]{1,0:T(8,128)(2,1)S(1)}, bf16[2048,256]{1,0:T(8,128)(2,1)S(1)}, u32[]{:S(2)}, u32[]{:S(2)}) collective-permute-start(bf16[2048,256]{1,0:T(8,128)(2,1)S(1)} %pad_maximum_fusion.7), channel_id=1, source_target_pairs={{0,8},{8,0},{16,24},{24,16},{1,9},{9,1},{17,25},{25,17},{2,10},{10... | collective-permute-start | bytes 3145736 | tf_op jit(solution)/shard_map/ppermute | solution.py:167
  196.3 40.9 %collective-permute-start.30 = (bf16[2048,256]{1,0:T(8,128)(2,1)S(1)}, bf16[2048,256]{1,0:T(8,128)(2,1)S(1)}, u32[]{:S(2)}, u32[]{:S(2)}) collective-permute-start(bf16[2048,256]{1,0:T(8,128)(2,1)S(1)} %collective-permute-done.29), channel_id=1, source_target_pairs={{0,8},{8,0},{16,24},{24,16},{1,9},{9,1},{17,25},{25,17},{2,10},{10... | collective-permute-start | bytes 3145736 | tf_op jit(solution)/shard_map/ppermute | solution.py:167
  223.0 76.6 %collective-permute-start.17 = (bf16[1024,512]{0,1:T(8,128)(2,1)S(1)}, bf16[1024,512]{0,1:T(8,128)(2,1)S(1)}, u32[]{:S(2)}, u32[]{:S(2)}) collective-permute-start(bf16[1024,512]{0,1:T(8,128)(2,1)S(1)} %pad_maximum_fusion.2), channel_id=1, source_target_pairs={{0,1},{1,0},{2,3},{3,2},{4,5},{5,4},{6,7},{7,6},{8,9},{9,8},{10,11... | collective-permute-start | bytes 3145736 | tf_op jit(solution)/shard_map/ppermute | solution.py:180
  230.5 55.0 %collective-permute-start.42 = (bf16[512,512]{0,1:T(8,128)(2,1)S(1)}, bf16[512,512]{0,1:T(8,128)(2,1)S(1)}, u32[]{:S(2)}, u32[]{:S(2)}) collective-permute-start(bf16[512,512]{0,1:T(8,128)(2,1)S(1)} %pad_maximum_fusion.11), channel_id=1, source_target_pairs={{0,1},{1,0},{2,3},{3,2},{4,5},{5,4},{6,7},{7,6},{8,9},{9,8},{10,11... | collective-permute-start | bytes 1572872 | tf_op jit(solution)/shard_map/ppermute | solution.py:180
  233.4 37.1 %collective-permute-start.38 = (bf16[512,512]{0,1:T(8,128)(2,1)S(1)}, bf16[512,512]{0,1:T(8,128)(2,1)S(1)}, u32[]{:S(2)}, u32[]{:S(2)}) collective-permute-start(bf16[512,512]{0,1:T(8,128)(2,1)S(1)} %pad_maximum_fusion.10), channel_id=1, source_target_pairs={{0,1},{1,0},{2,3},{3,2},{4,5},{5,4},{6,7},{7,6},{8,9},{9,8},{10,11... | collective-permute-start | bytes 1572872 | tf_op jit(solution)/shard_map/ppermute | solution.py:180
  291.5 31.5 %collective-permute-start.31 = (bf16[1024,512]{0,1:T(8,128)(2,1)S(1)}, bf16[1024,512]{0,1:T(8,128)(2,1)S(1)}, u32[]{:S(2)}, u32[]{:S(2)}) collective-permute-start(bf16[1024,512]{0,1:T(8,128)(2,1)S(1)} %pad_maximum_fusion.6), channel_id=1, source_target_pairs={{0,1},{1,0},{2,3},{3,2},{4,5},{5,4},{6,7},{7,6},{8,9},{9,8},{10,11... | collective-permute-start | bytes 3145736 | tf_op jit(solution)/shard_map/ppermute | solution.py:180
  300.3 28.0 %collective-permute-start.19 = (bf16[1024,128]{0,1:T(8,128)(2,1)S(1)}, bf16[1024,128]{0,1:T(8,128)(2,1)S(1)}, u32[]{:S(2)}, u32[]{:S(2)}) collective-permute-start(bf16[1024,128]{0,1:T(8,128)(2,1)S(1)} %get-tuple-element.23), channel_id=1, source_target_pairs={{0,4},{1,5},{2,6},{3,7},{4,0},{5,1},{6,2},{7,3},{8,12},{9,13},{10,... | collective-permute-start | bytes 786440 | tf_op jit(solution)/shard_map/ppermute | solution.py:190
  301.7 26.9 %collective-permute-start.20 = (bf16[1024,128]{0,1:T(8,128)(2,1)S(1)}, bf16[1024,128]{0,1:T(8,128)(2,1)S(1)}, u32[]{:S(2)}, u32[]{:S(2)}) collective-permute-start(bf16[1024,128]{0,1:T(8,128)(2,1)S(1)} %get-tuple-element.22), channel_id=1, source_target_pairs={{0,2},{1,3},{2,4},{3,5},{4,6},{5,7},{6,0},{7,1},{8,10},{9,11},{10,... | collective-permute-start | bytes 786440 | tf_op jit(solution)/shard_map/ppermute | solution.py:190
  305.1 37.5 %collective-permute-start.25 = (bf16[1024,128]{0,1:T(8,128)(2,1)S(1)}, bf16[1024,128]{0,1:T(8,128)(2,1)S(1)}, u32[]{:S(2)}, u32[]{:S(2)}) collective-permute-start(bf16[1024,128]{0,1:T(8,128)(2,1)S(1)} %get-tuple-element.24), channel_id=1, source_target_pairs={{0,6},{1,7},{2,0},{3,1},{4,2},{5,3},{6,4},{7,5},{8,14},{9,15},{10,... | collective-permute-start | bytes 786440 | tf_op jit(solution)/shard_map/ppermute | solution.py:190
  323.0 36.3 %collective-permute-start.26 = (bf16[1024,128]{0,1:T(8,128)(2,1)S(1)}, bf16[1024,128]{0,1:T(8,128)(2,1)S(1)}, u32[]{:S(2)}, u32[]{:S(2)}) collective-permute-start(bf16[1024,128]{0,1:T(8,128)(2,1)S(1)} %get-tuple-element.26), channel_id=1, source_target_pairs={{0,4},{1,5},{2,6},{3,7},{4,0},{5,1},{6,2},{7,3},{8,12},{9,13},{10,... | collective-permute-start | bytes 786440 | tf_op jit(solution)/shard_map/ppermute | solution.py:190
  324.6 34.7 %collective-permute-start.27 = (bf16[1024,128]{0,1:T(8,128)(2,1)S(1)}, bf16[1024,128]{0,1:T(8,128)(2,1)S(1)}, u32[]{:S(2)}, u32[]{:S(2)}) collective-permute-start(bf16[1024,128]{0,1:T(8,128)(2,1)S(1)} %get-tuple-element.25), channel_id=1, source_target_pairs={{0,2},{1,3},{2,4},{3,5},{4,6},{5,7},{6,0},{7,1},{8,10},{9,11},{10,... | collective-permute-start | bytes 786440 | tf_op jit(solution)/shard_map/ppermute | solution.py:190
  328.3 31.1 %collective-permute-start.32 = (bf16[1024,128]{0,1:T(8,128)(2,1)S(1)}, bf16[1024,128]{0,1:T(8,128)(2,1)S(1)}, u32[]{:S(2)}, u32[]{:S(2)}) collective-permute-start(bf16[1024,128]{0,1:T(8,128)(2,1)S(1)} %get-tuple-element.27), channel_id=1, source_target_pairs={{0,6},{1,7},{2,0},{3,1},{4,2},{5,3},{6,4},{7,5},{8,14},{9,15},{10,... | collective-permute-start | bytes 786440 | tf_op jit(solution)/shard_map/ppermute | solution.py:190
  328.6 41.2 %collective-permute-start.33 = (bf16[1024,128]{0,1:T(8,128)(2,1)S(1)}, bf16[1024,128]{0,1:T(8,128)(2,1)S(1)}, u32[]{:S(2)}, u32[]{:S(2)}) collective-permute-start(bf16[1024,128]{0,1:T(8,128)(2,1)S(1)} %get-tuple-element.29), channel_id=1, source_target_pairs={{0,4},{1,5},{2,6},{3,7},{4,0},{5,1},{6,2},{7,3},{8,12},{9,13},{10,... | collective-permute-start | bytes 786440 | tf_op jit(solution)/shard_map/ppermute | solution.py:190
  342.7 27.2 %collective-permute-start.34 = (bf16[1024,128]{0,1:T(8,128)(2,1)S(1)}, bf16[1024,128]{0,1:T(8,128)(2,1)S(1)}, u32[]{:S(2)}, u32[]{:S(2)}) collective-permute-start(bf16[1024,128]{0,1:T(8,128)(2,1)S(1)} %get-tuple-element.28), channel_id=1, source_target_pairs={{0,2},{1,3},{2,4},{3,5},{4,6},{5,7},{6,0},{7,1},{8,10},{9,11},{10,... | collective-permute-start | bytes 786440 | tf_op jit(solution)/shard_map/ppermute | solution.py:190
  (64 other events, 1548.7 us)

commit v2 on v0

v2 whole, which is shorter than its diff:
```python
import functools

import jax
import jax.numpy as jnp
from jax import lax
from jax.experimental import pallas as pl
from jax.experimental.pallas import tpu as pltpu
from jax.sharding import PartitionSpec as P

IMAGES = 2
GRIDW = 64
BAND = IMAGES * GRIDW
CORES = 2
LANES = 128
TILES = 4
SPLITS = 2
MM_VMEM = 60 << 20
MM_ROWS = 512


def mm_kernel(places, homes, base, start_ref, bias_ref, *refs):
    many = max(i for tile_homes in homes for i, _ in tile_homes) + 1
    toks, weights = refs[:len(places)], refs[len(places):len(places) + many]
    out, first, final, tok, held, stage, acc, tsem, wsem, osem = refs[-10:]
    nz, rows, _ = tok.shape
    _, tile = held.shape[2:]
    nx = start_ref.shape[0] - nz

    def tok_copy(i):
        row, s, k = places[i]
        n, width = toks[i].shape
        col = pl.multiple_of(start_ref[k], width)
        return pltpu.make_async_copy(toks[i], tok.at[s, pl.ds(row, n), pl.ds(col, width)], tsem.at[i])

    def weight_copy(t, r):
        ref, col = homes[t][r]
        slot = start_ref[nx + r]
        return pltpu.make_async_copy(weights[ref].at[:, pl.ds(col, tile)], held.at[t % 2, slot], wsem.at[t % 2, slot])

    def weight_wait(t, s):
        pltpu.make_async_copy(weights[0].at[:, pl.ds(0, tile)], held.at[t % 2, s], wsem.at[t % 2, s]).wait()

    def out_copies(t):
        cols = pl.ds(t * tile, tile)
        kept = stage.at[t % 2]
        return [
            pltpu.make_async_copy(kept, out.at[:, pl.ds((base + t) * tile, tile)], osem.at[t % 2, 0]),
            pltpu.make_async_copy(kept.at[pl.ds(0, BAND)], first.at[:, cols], osem.at[t % 2, 1]),
            pltpu.make_async_copy(kept.at[pl.ds(rows - BAND, BAND)], final.at[:, cols], osem.at[t % 2, 2]),
        ]

    tiles = len(homes)
    step = min(MM_ROWS, rows)
    by_slot = [[i for i in range(len(places)) if places[i][1] == s] for s in range(nz)]
    for i in by_slot[0]:
        tok_copy(i).start()
    for r in range(nz):
        weight_copy(0, r).start()
    for s in range(1, nz):
        for i in by_slot[s]:
            tok_copy(i).start()
    for t in range(tiles):
        if t + 1 < tiles:
            for r in range(nz):
                weight_copy(t + 1, r).start()
        if t >= 2:
            for copy in out_copies(t - 2):
                copy.wait()
        for group in ([[s] for s in range(nz)] if t == 0 else [list(range(nz))]):
            for s in group:
                if t == 0:
                    for i in by_slot[s]:
                        tok_copy(i).wait()
                weight_wait(t, s)

            def body(m, _, group=group, t=t):
                at = pl.ds(pl.multiple_of(m * step, step), step)
                if group[0] == 0:
                    total = bias_ref[:, (base + t) * tile:(base + t + 1) * tile] + jnp.zeros((step, tile), jnp.float32)
                else:
                    total = acc[at, :]
                for s in group:
                    total = total + jnp.dot(tok[s, at, :], held[t % 2, s], preferred_element_type=jnp.float32)
                if group[-1] == nz - 1:
                    stage[t % 2, at, :] = total.astype(stage.dtype)
                else:
                    acc[at, :] = total
                return 0

            lax.fori_loop(0, rows // step, body, 0)
        for copy in out_copies(t):
            copy.start()
    for t in range(max(0, tiles - 2), tiles):
        for copy in out_copies(t):
            copy.wait()


def project(starts, bias, toks, places, weights, homes, base, old, rows, depth, tile, nz):
    part = tile * len(homes)
    anywhere = pl.BlockSpec(memory_space=pl.ANY)
    return pl.pallas_call(
        functools.partial(mm_kernel, places, homes, base),
        in_specs=[pl.BlockSpec(memory_space=pltpu.SMEM), pl.BlockSpec(memory_space=pltpu.VMEM)]
        + [anywhere] * (len(toks) + len(weights) + len(old)),
        out_specs=[anywhere] * 3,
        out_shape=[jax.ShapeDtypeStruct(dims, jnp.bfloat16) for dims in ((rows, bias.shape[0]), (BAND, part), (BAND, part))],
        input_output_aliases={2 + len(toks) + len(weights) + i: i for i in range(len(old))},
        scratch_shapes=[
            pltpu.VMEM((nz, rows, depth), jnp.bfloat16),
            pltpu.VMEM((2, nz, depth, tile), jnp.bfloat16),
            pltpu.VMEM((2, rows, tile), jnp.bfloat16),
            pltpu.VMEM((rows, tile), jnp.float32),
            pltpu.SemaphoreType.DMA((len(toks),)),
            pltpu.SemaphoreType.DMA((2, nz)),
            pltpu.SemaphoreType.DMA((2, 3)),
        ],
        compiler_params=pltpu.CompilerParams(vmem_limit_bytes=MM_VMEM),
        cost_estimate=pl.CostEstimate(flops=2 * rows * nz * depth * part, bytes_accessed=2 * nz * depth * (rows + part), transcendentals=0),
    )(starts, bias[None], *toks, *weights, *old)


def conv_kernel(parts, pre_ref, *refs):
    n = len(parts)
    taps_ref, bias_ref, out_ref, left, right = refs[2 * n:]
    for f, (lo, hi) in enumerate(parts):
        inside = (pl.program_id(0) >= lo) & (pl.program_id(0) < hi)
        pl.when(inside)(functools.partial(conv_tile, pre_ref, refs[f], refs[n + f], taps_ref, bias_ref, out_ref, left, right))


def conv_tile(pre_ref, before_ref, after_ref, taps_ref, bias_ref, out_ref, left, right):
    rows, tile = out_ref.shape
    height = rows // BAND

    def body(n, _):
        lanes = pl.ds(pl.multiple_of(n // IMAGES * LANES, LANES), LANES)
        first = n % IMAGES * GRIDW
        taps = [taps_ref[i:i + 1, lanes] for i in range(9)]
        bias = bias_ref[:, lanes]
        left[7:8] = jnp.zeros((1, LANES), jnp.float32)
        right[GRIDW:GRIDW + 1] = jnp.zeros((1, LANES), jnp.float32)

        def row(h):
            ref, base = pre_ref, h * BAND
            if h < 0:
                ref, base = before_ref, 0
            if h >= height:
                ref, base = after_ref, 0
            at = pl.ds(pl.multiple_of(first + base, GRIDW), GRIDW)
            return ref[at, lanes].astype(jnp.float32)

        above, here = row(-1), row(0)
        for h in range(height):
            below = row(h + 1)
            left[8:8 + GRIDW] = above * taps[0] + here * taps[3] + below * taps[6]
            right[0:GRIDW] = above * taps[2] + here * taps[5] + below * taps[8]
            conv = bias + (above * taps[1] + here * taps[4] + below * taps[7])
            conv = conv + left[7:7 + GRIDW] + right[1:1 + GRIDW]
            act = 0.5 * conv * (1.0 + lax.erf(conv * 0.5 ** 0.5))
            at = pl.ds(pl.multiple_of(first + h * BAND, GRIDW), GRIDW)
            out_ref[at, lanes] = act.astype(out_ref.dtype)
            above, here = here, below
        return 0

    lax.fori_loop(0, IMAGES * (tile // LANES), body, 0)


def convolve(pre, befores, afters, taps, bias, tile, parts):
    rows, hidden = pre.shape

    def wide(n):
        return pl.BlockSpec((n, tile), lambda i: (0, i))

    edges = [pl.BlockSpec((BAND, tile), lambda i, lo=lo, hi=hi: (0, jnp.clip(i - lo, 0, hi - lo - 1))) for lo, hi in parts]
    return pl.pallas_call(
        functools.partial(conv_kernel, parts),
        grid=(hidden // tile,),
        in_specs=[wide(rows)] + edges + edges + [wide(9), wide(1)],
        out_specs=wide(rows),
        out_shape=jax.ShapeDtypeStruct((rows, hidden), jnp.bfloat16),
        scratch_shapes=[pltpu.VMEM((GRIDW + 16, LANES), jnp.float32)] * 2,
        compiler_params=pltpu.CompilerParams(vmem_limit_bytes=24 << 20),
        cost_estimate=pl.CostEstimate(flops=60 * rows * hidden, bytes_accessed=4 * rows * hidden, transcendentals=0),
    )(pre, *befores, *afters, taps, bias[None])


def local(tokens, w_in, b_in, dw_kernel, dw_bias, w_out, b_out):
    nt, nc = lax.axis_size("tok"), lax.axis_size("ch")
    nz, nx, ny = nt, nc // nt, nt // CORES
    t, c = lax.axis_index("tok"), lax.axis_index("ch")
    z, x = c // nx, c % nx
    y, core = t // CORES, t % CORES
    rows, width = tokens.shape
    depth, hidden = w_in.shape
    tile = hidden // TILES
    parts = [(0, TILES - 1), (TILES - 1, TILES)]
    half = rows // 2

    def zshift(k):
        return [(i, (i + k * nx) % nc) for i in range(nc)]

    def xshift(k):
        return [(i, i // nx * nx + (i + k) % nx) for i in range(nc)]

    def yshift(k):
        return [(i, (i + CORES * k) % nt) for i in range(nt)]

    swap = [(i, i ^ 1) for i in range(nt)]

    def owner(k, other):
        return (y + ny - k) % ny * CORES + (1 - core if other else core)

    toks, places, across = [], [], []
    for s in range(nz):
        if s == 0:
            held = [tokens]
        elif s == 1:
            held = [lax.ppermute(tokens, "ch", zshift(1))]
        else:
            held = held if len(held) == 2 else [held[0][:half], held[0][half:]]
            held = [lax.ppermute(held[h], "ch", zshift(1)) for h in range(2)]
        across.append({})
        for h, block in enumerate(held):
            toks.append(block)
            places.append((h * half, s, 0))
            for k in range(1, nx):
                if s == nz - 1 and h == 1:
                    got = lax.ppermute(across[s - 1][h, k], "ch", zshift(1))
                else:
                    got = lax.ppermute(block, "ch", xshift(k))
                across[s][h, k] = got
                toks.append(got)
                places.append((h * half, s, k))

    starts = [(x + nx - k) % nx * width for k in range(nx)]
    starts += [(z + nz - owner(k, other)) % nz for k in range(ny) for other in (0, 1)]
    starts = jnp.stack(starts).astype(jnp.int32)
    partner = lax.ppermute(w_in, "tok", swap)
    pieces_in = []
    for n in range(TILES):
        row = []
        for k in range(1, ny):
            mine = lax.ppermute(w_in[:, n * tile:(n + 1) * tile], "tok", yshift(k))
            row += [mine, lax.ppermute(mine, "tok", swap)]
        pieces_in.append(row)
    up = [(i, i + 1) for i in range(nt - 1)]
    down = [(i + 1, i) for i in range(nt - 1)]
    pre, befores, afters = [], [], []
    for lo, hi in parts:
        weights, homes = [w_in, partner], []
        for n in range(lo, hi):
            homes.append([(0, n * tile), (1, n * tile)] + [(len(weights) + i, 0) for i in range(nt - 2)])
            weights += pieces_in[n]
        out, first, final = project(starts, b_in, toks, places, weights, homes, lo, pre, rows, depth, tile, nz)
        pre = [out]
        afters.append(lax.ppermute(first, "tok", down))
        befores.append(lax.ppermute(final, "tok", up))
    act = convolve(pre[0], befores, afters, dw_kernel, dw_bias, tile, parts)

    pieces = max(1, width // LANES)
    cols = width // pieces
    partner_out = lax.ppermute(w_out, "tok", swap)
    outs = []
    behind = None
    for q in range(pieces):

        def cut_of(array):
            return [lax.dynamic_slice_in_dim(array, (x + k) % nx * width + q * cols, cols, 1) for k in range(nx)]

        order = list(range(1, nx)) + [0]
        own = cut_of(w_out)
        joint = jnp.concatenate([own[k] for k in order], axis=1)
        theirs = cut_of(partner_out)
        near = [joint, jnp.concatenate([theirs[k] for k in order], axis=1)]
        near = [jnp.dot(act, b, preferred_element_type=jnp.float32).astype(jnp.bfloat16) for b in near]
        apart = q in (0, pieces - 1)
        groups = [[k] for k in order] if apart else [order]
        far = {}
        for group in groups:
            block = own[group[0]] if apart else joint
            for j in range(1, ny):
                mine = lax.ppermute(block, "tok", yshift(j))
                pair = lax.ppermute(mine, "tok", swap)
                dots = [jnp.dot(act, b, preferred_element_type=jnp.float32).astype(jnp.bfloat16) for b in (mine, pair)]
                for i, k in enumerate(group):
                    far.setdefault(k, [])
                    far[k] += [d[:, i * cols:(i + 1) * cols] for d in dots]

        def shares(k, cut):
            i = order.index(k)
            return jnp.concatenate([d[cut, i * cols:(i + 1) * cols] for d in near] + [d[cut] for d in far[k]], axis=1)

        step = rows // SPLITS
        bands = []
        for h in range(SPLITS):
            cut = slice(h * step, (h + 1) * step)
            depth_first = h == 1 and q == 0
            if depth_first:
                totals = [shares(k, cut) for k in range(nx)]
            else:
                arrived = [lax.ppermute(shares(k, cut), "ch", xshift(k)) for k in range(1, nx)]
                if behind is not None:
                    arrived, _ = lax.optimization_barrier((arrived, behind))
                total = shares(0, cut).astype(jnp.float32)
                for got in arrived:
                    total = total + got.astype(jnp.float32)
                totals = [total]

            def term(goal):
                at = (y + ny - goal // CORES) % ny * CORES + (goal + core) % CORES
                return jnp.concatenate([lax.dynamic_slice_in_dim(v, at * cols, cols, 1) for v in totals], axis=1)

            live = {j: term(z ^ j) for j in range(nz)}
            span = live[0].shape[1]
            bit = 1
            while bit < nz:
                away = [j for j in live if j & bit]
                packed = jnp.concatenate([live.pop(j).astype(jnp.bfloat16) for j in away], axis=1)
                if bit == 1 and not depth_first:
                    behind = packed
                got = lax.ppermute(packed, "ch", [(i, (i // nx ^ bit) * nx + i % nx) for i in range(nc)])
                for i, j in enumerate(away):
                    more = got[:, i * span:(i + 1) * span].astype(jnp.float32)
                    live[j ^ bit] = live[j ^ bit].astype(jnp.float32) + more
                bit *= 2
            if depth_first:
                mine = live[0][:, :cols]
                for k in range(1, nx):
                    away = live[0][:, k * cols:(k + 1) * cols].astype(jnp.bfloat16)
                    mine = mine + lax.ppermute(away, "ch", xshift(k)).astype(jnp.float32)
                live[0] = mine
            bands.append(live[0])
        outs.append(jnp.concatenate(bands, axis=0))
    return (jnp.concatenate(outs, axis=1) + b_out).astype(jnp.bfloat16)


def solution(mesh):
    in_specs = (
        P("tok", "ch"),
        P("tok", "ch"),
        P("ch"),
        P(None, "ch"),
        P("ch"),
        P("ch", "tok"),
        P("ch"),
    )
    return jax.shard_map(local, mesh=mesh, in_specs=in_specs, out_specs=P("tok", "ch"), check_vma=False)
```

time: 669 us -> 409 us (0.61); the launches traced: 669 us -> 401 us
  waiting for transfers between devices: 574 us -> 246 us
  starting transfers between devices: 4.47 us -> 63.5 us
  Pallas kernels: 0 us -> 39.4 us
  other arithmetic: 31.1 us -> 4.6 us
  matrix products: 46.1 us -> 33.1 us
  local copies, waits for them, and re-layouts: 0.17 us -> 11.9 us
  between operations: 13.2 us -> 1.83 us
    all_gather x3 -> x0, waiting for transfers between devices: 290 us -> none  [the longest x1 128 us: local(): lax.all_gather(tokens, 'ch', axis=1, tiled=True)]
    reduce_scatter x1 -> x0, waiting for transfers between devices: 280 us -> none  [local(): lax.psum_scatter(lax.dot_general(w_cols, act, (((0,), (1,)), ((), ())), p...]
    ppermute x2 -> x61, waiting for transfers between devices: 1.88 us -> 246 us  [the longest x16 55.9 us: local(): lax.ppermute(packed, 'ch', [(i, (i // nx ^ bit) * nx + i % nx) for i in r...]
    ppermute x2 -> x61, starting transfers between devices: 4.36 us -> 63.5 us  [the longest x16 13.9 us: local(): lax.ppermute(packed, 'ch', [(i, (i // nx ^ bit) * nx + i % nx) for i in r...]
    pallas_call x0 -> x3, Pallas kernels: none -> 39.4 us  [the longest x2 30.2 us: project(): pl.pallas_call(functools.partial(mm_kernel, places, homes, base), in_spec...]
    convert_element_type x3 -> x9, other arithmetic: 31.1 us -> 0.48 us  [the longest x8 0.3 us: local(): live.pop(j).astype(jnp.bfloat16)]
    dot_general x2 -> x20, matrix products: 46.1 us -> 33.1 us  [local(): jnp.dot(act, b, preferred_element_type=jnp.float32).astype(jnp.bfloat16)]
  transfers between devices with their start and end apart: 6 -> 61, of which waited for: 5 -> 30; matrix products, arithmetic and copies ran while one was open for 8% -> 12% of each run, Pallas kernels for 0% -> 10%
where the time goes in v2:
time: 409 us; the launch traced here: 401 us
  waiting for transfers between devices  246 us (60%)
  starting transfers between devices  63.5 us (16%)
  Pallas kernels  39.4 us (10%)
  matrix products  33.1 us (8%)
  local copies, waits for them, and re-layouts  11.9 us (3%)
  other arithmetic  4.6 us (1%)
    ppermute x16, waiting for transfers between devices, local(): lax.ppermute(packed, 'ch', [(i, (i // nx ^ bit) * nx + i % nx) for i in r...  55.9 us
    ppermute x4, waiting for transfers between devices, local(): mine = lax.ppermute(w_in[:, n * tile:(n + 1) * tile], 'tok', yshift(k))  51.4 us
    ppermute x7, waiting for transfers between devices, local(): lax.ppermute(shares(k, cut), 'ch', xshift(k))  40.3 us
    dot_general x20, matrix products, local(): jnp.dot(act, b, preferred_element_type=jnp.float32).astype(jnp.bfloat16)  33.1 us
    ppermute x5, waiting for transfers between devices, local(): got = lax.ppermute(block, 'ch', xshift(k))  32.7 us
    pallas_call x2, Pallas kernels, project(): pl.pallas_call(functools.partial(mm_kernel, places, homes, base), in_spec...  30.2 us
    ppermute x2, waiting for transfers between devices, local(): afters.append(lax.ppermute(first, 'tok', down))  23 us
    ppermute x1, waiting for transfers between devices, local(): held = [lax.ppermute(tokens, 'ch', zshift(1))]  19.4 us
  transfers between devices with their start and end apart: 61, of which 30 were waited for; matrix products, arithmetic and copies ran while one was open for 12% of the time, Pallas kernels for 10%

profile of v2, /device:TPU:0, one launch (start us, length us, event | category | flops | bytes accessed | tf_op | source)
XLA Modules:
  0.0 400.7 jit_solution(16919473320199850389)
XLA Ops:
  0.0 3.1 collective-permute-start.1
  9.1 19.4 %collective-permute-done.1.refs_2_ = bf16[1024,512]{1,0:T(8,128)(2,1)S(1)} collective-permute-done((bf16[1024,512]{1,0:T(8,128)(2,1)}, bf16[1024,512]{1,0:T(8,128)(2,1)S(1)}, u32[]{:S(2)}, u32[]{:S(2)}) %collective-permute-start.1) | collective-permute-done | bytes 1048608 | tf_op jit(solution)/shard_map/ppermute | solution.py:217
  33.1 20.9 %collective-permute-done.16.refs_16_ = bf16[1024,512]{1,0:T(8,128)(2,1)S(1)} collective-permute-done((bf16[1024,512]{1,0:T(8,128)(2,1)S(1)}, bf16[1024,512]{1,0:T(8,128)(2,1)S(1)}, u32[]{:S(2)}, u32[]{:S(2)}) %collective-permute-start.16) | collective-permute-done | bytes 1048608 | tf_op jit(solution)/shard_map/ppermute | solution.py:242
  55.7 21.0 %collective-permute-done.18.refs_18_ = bf16[1024,512]{1,0:T(8,128)(2,1)} collective-permute-done((bf16[1024,512]{1,0:T(8,128)(2,1)S(1)}, bf16[1024,512]{1,0:T(8,128)(2,1)}, u32[]{:S(2)}, u32[]{:S(2)}) %collective-permute-start.18) | collective-permute-done | bytes 1048608 | tf_op jit(solution)/shard_map/ppermute | solution.py:242
  79.7 9.8 %collective-permute-done.3.refs_4_ = bf16[512,512]{1,0:T(8,128)(2,1)S(1)} collective-permute-done((bf16[512,512]{1,0:T(8,128)(2,1)S(1)}, bf16[512,512]{1,0:T(8,128)(2,1)S(1)}, u32[]{:S(2)}, u32[]{:S(2)}) %collective-permute-start.3) | collective-permute-done | bytes 524320 | tf_op jit(solution)/shard_map/ppermute | solution.py:220
  89.8 7.9 %collective-permute-done.12.refs_14_ = bf16[1024,512]{1,0:T(8,128)(2,1)} collective-permute-done((bf16[1024,512]{1,0:T(8,128)(2,1)S(1)}, bf16[1024,512]{1,0:T(8,128)(2,1)}, u32[]{:S(2)}, u32[]{:S(2)}) %collective-permute-start.12) | collective-permute-done | bytes 1048608 | tf_op jit(solution)/shard_map/ppermute | solution.py:242
  101.8 8.5 %collective-permute-done.4.refs_5_ = bf16[512,512]{1,0:T(8,128)(2,1)S(1)} collective-permute-done((bf16[512,512]{1,0:T(8,128)(2,1)S(1)}, bf16[512,512]{1,0:T(8,128)(2,1)S(1)}, u32[]{:S(2)}, u32[]{:S(2)}) %collective-permute-start.4) | collective-permute-done | bytes 524320 | tf_op jit(solution)/shard_map/ppermute | solution.py:229
  110.3 3.0 collective-permute-done.9.refs_10_
  117.4 3.7 constant_dynamic-slice_fusion.22
  124.1 15.5 %collective-permute-done.2.refs_3_ = bf16[1024,512]{1,0:T(8,128)(2,1)} collective-permute-done((bf16[1024,512]{1,0:T(8,128)(2,1)S(1)}, bf16[1024,512]{1,0:T(8,128)(2,1)}, u32[]{:S(2)}, u32[]{:S(2)}) %collective-permute-start.2) | collective-permute-done | bytes 1048608 | tf_op jit(solution)/shard_map/ppermute | solution.py:229
  141.5 8.7 %collective-permute-done.8.refs_9_ = bf16[512,512]{1,0:T(8,128)(2,1)} collective-permute-done((bf16[512,512]{1,0:T(8,128)(2,1)}, bf16[512,512]{1,0:T(8,128)(2,1)}, u32[]{:S(2)}, u32[]{:S(2)}) %collective-permute-start.8) | collective-permute-done | bytes 524320 | tf_op jit(solution)/shard_map/ppermute | solution.py:229
  151.8 19.3 %shard_map.73 = (bf16[1024,2048]{1,0:T(8,128)(2,1)}, bf16[128,1536]{1,0:T(8,128)(2,1)}, bf16[128,1536]{1,0:T(8,128)(2,1)}) custom-call(s32[6]{0:T(128)} %stack.27.start_ref, f32[1,2048]{1,0:T(1,128)} %bitcast.41, bf16[1024,512]{1,0:T(8,128)(2,1)} %refs_0_.3, bf16[1024,512]{1,0:T(8,128)(2,1)} %copy-done.7, bf16[1024,512]{1,0:T(8,128)(2,1)} %copy-done.3, ...), custom_call_target="tpu_custom_call" | custom-call | flops 12884901888 | bytes 20971520 | tf_op jit(solution)/shard_map/pallas_call | solution.py:101
  176.7 10.9 %shard_map.74 = (bf16[1024,2048]{1,0:T(8,128)(2,1)}, bf16[128,512]{1,0:T(8,128)(2,1)}, bf16[128,512]{1,0:T(8,128)(2,1)}) custom-call(s32[6]{0:T(128)} %stack.27.start_ref, f32[1,2048]{1,0:T(1,128)} %bitcast.42, bf16[1024,512]{1,0:T(8,128)(2,1)} %refs_0_.3, bf16[1024,512]{1,0:T(8,128)(2,1)} %copy-done.7, ...), custom_call_target="tpu_custom_call", output_to_operand_aliasing={{0}: (18, {})} | custom-call | flops 4294967296 | bytes 12582912 | tf_op jit(solution)/shard_map/pallas_call | solution.py:101
  187.6 3.5 collective-permute-start.21
  193.8 23.0 %collective-permute-done.23.refs_3_ = bf16[128,512]{1,0:T(8,128)(2,1)S(1)} collective-permute-done((bf16[128,512]{1,0:T(8,128)(2,1)}, bf16[128,512]{1,0:T(8,128)(2,1)S(1)}, u32[]{:S(2)}, u32[]{:S(2)}) %collective-permute-start.23) | collective-permute-done | bytes 131104 | tf_op jit(solution)/shard_map/ppermute | solution.py:255
  216.7 4.0 %collective-permute-start.53 = (bf16[2048,128]{1,0:T(8,128)(2,1)}, bf16[2048,128]{1,0:T(8,128)(2,1)S(1)}, u32[]{:S(2)}, u32[]{:S(2)}) collective-permute-start(bf16[2048,128]{1,0:T(8,128)(2,1)} %get-tuple-element.36), channel_id=1, source_target_pairs={{0,16},{8,24},{16,0},{24,8},{1,17},{9,25},{17,1},{25,9},{2,18},{10... | collective-permute-start | bytes 1572872 | tf_op jit(solution)/shard_map/ppermute | solution.py:281
  225.1 9.2 %shard_map.75 = bf16[1024,2048]{1,0:T(8,128)(2,1)S(1)} custom-call(bf16[1024,2048]{1,0:T(8,128)(2,1)S(1)} %copy-done, bf16[128,1536]{1,0:T(8,128)(2,1)S(1)} %collective-permute-done.20.refs_0_, bf16[128,512]{1,0:T(8,128)(2,1)S(1)} %collective-permute-done.21.refs_1_, bf16[128,1536]{1,0:T(8,128)(2,1)S(1)} %collective-permute-done.22.refs_2_, ...), custom_call_target="tpu_custom_call" | custom-call | flops 125829120 | bytes 8388608 | tf_op jit(solution)/shard_map/pallas_call | solution.py:174
  237.0 7.1 %collective-permute-done.51 = bf16[2048,128]{1,0:T(8,128)(2,1)S(1)} collective-permute-done((bf16[2048,128]{1,0:T(8,128)(2,1)}, bf16[2048,128]{1,0:T(8,128)(2,1)S(1)}, u32[]{:S(2)}, u32[]{:S(2)}) %collective-permute-start.51) | collective-permute-done | bytes 524320 | tf_op jit(solution)/shard_map/ppermute | solution.py:281
  284.5 4.2 %collective-permute-done.40 = bf16[512,512]{0,1:T(8,128)(2,1)S(1)} collective-permute-done((bf16[512,512]{0,1:T(8,128)(2,1)S(1)}, bf16[512,512]{0,1:T(8,128)(2,1)S(1)}, u32[]{:S(2)}, u32[]{:S(2)}) %collective-permute-start.40) | collective-permute-done | bytes 524320 | tf_op jit(solution)/shard_map/ppermute | solution.py:300
  289.8 10.1 %collective-permute-done.45 = bf16[512,512]{0,1:T(8,128)(2,1)S(1)} collective-permute-done((bf16[512,512]{0,1:T(8,128)(2,1)S(1)}, bf16[512,512]{0,1:T(8,128)(2,1)S(1)}, u32[]{:S(2)}, u32[]{:S(2)}) %collective-permute-start.45) | collective-permute-done | bytes 524320 | tf_op jit(solution)/shard_map/ppermute | solution.py:300
  302.2 9.0 %collective-permute-done.48 = bf16[512,512]{0,1:T(8,128)(2,1)S(1)} collective-permute-done((bf16[512,512]{0,1:T(8,128)(2,1)S(1)}, bf16[512,512]{0,1:T(8,128)(2,1)S(1)}, u32[]{:S(2)}, u32[]{:S(2)}) %collective-permute-start.48) | collective-permute-done | bytes 524320 | tf_op jit(solution)/shard_map/ppermute | solution.py:300
  313.4 9.0 %collective-permute-done.55 = bf16[512,512]{0,1:T(8,128)(2,1)S(1)} collective-permute-done((bf16[512,512]{0,1:T(8,128)(2,1)S(1)}, bf16[512,512]{0,1:T(8,128)(2,1)S(1)}, u32[]{:S(2)}, u32[]{:S(2)}) %collective-permute-start.55) | collective-permute-done | bytes 524320 | tf_op jit(solution)/shard_map/ppermute | solution.py:300
  324.8 8.0 %collective-permute-done.58 = bf16[512,512]{0,1:T(8,128)(2,1)S(1)} collective-permute-done((bf16[512,512]{0,1:T(8,128)(2,1)S(1)}, bf16[512,512]{0,1:T(8,128)(2,1)S(1)}, u32[]{:S(2)}, u32[]{:S(2)}) %collective-permute-start.58) | collective-permute-done | bytes 524320 | tf_op jit(solution)/shard_map/ppermute | solution.py:300
  333.8 13.1 %collective-permute-done.33 = bf16[512,256]{0,1:T(8,128)(2,1)S(1)} collective-permute-done((bf16[512,256]{0,1:T(8,128)(2,1)S(1)}, bf16[512,256]{0,1:T(8,128)(2,1)S(1)}, u32[]{:S(2)}, u32[]{:S(2)}) %collective-permute-start.33) | collective-permute-done | bytes 262176 | tf_op jit(solution)/shard_map/ppermute | solution.py:320
  352.6 7.7 %collective-permute-done.49 = bf16[512,256]{0,1:T(8,128)(2,1)S(1)} collective-permute-done((bf16[512,256]{0,1:T(8,128)(2,1)S(1)}, bf16[512,256]{0,1:T(8,128)(2,1)S(1)}, u32[]{:S(2)}, u32[]{:S(2)}) %collective-permute-start.49) | collective-permute-done | bytes 262176 | tf_op jit(solution)/shard_map/ppermute | solution.py:320
  360.3 6.5 %collective-permute-done.56 = bf16[512,256]{0,1:T(8,128)(2,1)S(1)} collective-permute-done((bf16[512,256]{0,1:T(8,128)(2,1)S(1)}, bf16[512,256]{0,1:T(8,128)(2,1)S(1)}, u32[]{:S(2)}, u32[]{:S(2)}) %collective-permute-start.56) | collective-permute-done | bytes 262176 | tf_op jit(solution)/shard_map/ppermute | solution.py:320
  366.9 3.7 collective-permute-done.59
  370.7 3.0 collective-permute-start.50
  373.8 10.5 %collective-permute-done.39 = bf16[512,128]{0,1:T(8,128)(2,1)S(1)} collective-permute-done((bf16[512,128]{0,1:T(8,128)(2,1)S(1)}, bf16[512,128]{0,1:T(8,128)(2,1)S(1)}, u32[]{:S(2)}, u32[]{:S(2)}) %collective-permute-start.39) | collective-permute-done | bytes 131104 | tf_op jit(solution)/shard_map/ppermute | solution.py:320
  387.2 4.2 %collective-permute-done.47 = bf16[512,128]{0,1:T(8,128)(2,1)S(1)} collective-permute-done((bf16[512,128]{0,1:T(8,128)(2,1)S(1)}, bf16[512,128]{0,1:T(8,128)(2,1)S(1)}, u32[]{:S(2)}, u32[]{:S(2)}) %collective-permute-start.47) | collective-permute-done | bytes 131104 | tf_op jit(solution)/shard_map/ppermute | solution.py:320
  391.4 2.8 collective-permute-done.50
  394.2 2.8 collective-permute-done.57
  (231 shorter events, 105.9 us)
Async XLA Ops:
  0.0 28.5 %collective-permute-start.1 = (bf16[1024,512]{1,0:T(8,128)(2,1)}, bf16[1024,512]{1,0:T(8,128)(2,1)S(1)}, u32[]{:S(2)}, u32[]{:S(2)}) collective-permute-start(bf16[1024,512]{1,0:T(8,128)(2,1)} %refs_0_.3), channel_id=1, source_target_pairs={{0,2},{1,3},{2,4},{3,5},{4,6},{5,7},{6,0},{7,1},{8,10},{9,11},{10,... | collective-permute-start | bytes 3145736 | tf_op jit(solution)/shard_map/ppermute | solution.py:217
  5.5 26.1 %collective-permute-start.14 = (bf16[1024,512]{1,0:T(8,128)(2,1)S(1)}, bf16[1024,512]{1,0:T(8,128)(2,1)S(1)}, u32[]{:S(2)}, u32[]{:S(2)}) collective-permute-start(bf16[1024,512]{1,0:T(8,128)(2,1)S(1)} %get-tuple-element.47), channel_id=1, source_target_pairs={{0,16},{8,24},{16,0},{24,8},{1,17},{9,25},{17,1},{25,9},{2,18},{10... | collective-permute-start | bytes 3145736 | tf_op jit(solution)/shard_map/ppermute | solution.py:242
  7.1 47.0 %collective-permute-start.16 = (bf16[1024,512]{1,0:T(8,128)(2,1)S(1)}, bf16[1024,512]{1,0:T(8,128)(2,1)S(1)}, u32[]{:S(2)}, u32[]{:S(2)}) collective-permute-start(bf16[1024,512]{1,0:T(8,128)(2,1)S(1)} %get-tuple-element.46), channel_id=1, source_target_pairs={{0,16},{8,24},{16,0},{24,8},{1,17},{9,25},{17,1},{25,9},{2,18},{10... | collective-permute-start | bytes 3145736 | tf_op jit(solution)/shard_map/ppermute | solution.py:242
  7.6 69.0 %collective-permute-start.18 = (bf16[1024,512]{1,0:T(8,128)(2,1)S(1)}, bf16[1024,512]{1,0:T(8,128)(2,1)}, u32[]{:S(2)}, u32[]{:S(2)}) collective-permute-start(bf16[1024,512]{1,0:T(8,128)(2,1)S(1)} %get-tuple-element.45), channel_id=1, source_target_pairs={{0,16},{8,24},{16,0},{24,8},{1,17},{9,25},{17,1},{25,9},{2,18},{10... | collective-permute-start | bytes 3145736 | tf_op jit(solution)/shard_map/ppermute | solution.py:242
  9.1 142.7 %collective-permute-start.11 = (bf16[1024,2048]{1,0:T(8,128)(2,1)}, bf16[1024,2048]{1,0:T(8,128)(2,1)}, u32[]{:S(2)}, u32[]{:S(2)}) collective-permute-start(bf16[1024,2048]{1,0:T(8,128)(2,1)} %refs_12_.3), channel_id=1, source_target_pairs={{0,8},{8,0},{16,24},{24,16},{1,9},{9,1},{17,25},{25,17},{2,10},{10... | collective-permute-start | bytes 12582920 | tf_op jit(solution)/shard_map/ppermute | solution.py:237
  28.5 61.3 %collective-permute-start = (bf16[1024,512]{1,0:T(8,128)(2,1)S(1)}, bf16[1024,512]{1,0:T(8,128)(2,1)S(1)}, u32[]{:S(2)}, u32[]{:S(2)}) collective-permute-start(bf16[1024,512]{1,0:T(8,128)(2,1)S(1)} %copy-done.6), channel_id=1, source_target_pairs={{0,1},{1,0},{2,3},{3,2},{4,5},{5,4},{6,7},{7,6},{8,9},{9,8},{10,11... | collective-permute-start | bytes 3145736 | tf_op jit(solution)/shard_map/ppermute | solution.py:229
  31.6 66.1 %collective-permute-start.12 = (bf16[1024,512]{1,0:T(8,128)(2,1)S(1)}, bf16[1024,512]{1,0:T(8,128)(2,1)}, u32[]{:S(2)}, u32[]{:S(2)}) collective-permute-start(bf16[1024,512]{1,0:T(8,128)(2,1)S(1)} %get-tuple-element.48), channel_id=1, source_target_pairs={{0,16},{8,24},{16,0},{24,8},{1,17},{9,25},{17,1},{25,9},{2,18},{10... | collective-permute-start | bytes 3145736 | tf_op jit(solution)/shard_map/ppermute | solution.py:242
  54.1 24.2 %collective-permute-start.5 = (bf16[512,512]{1,0:T(8,128)(2,1)S(1)}, bf16[512,512]{1,0:T(8,128)(2,1)S(1)}, u32[]{:S(2)}, u32[]{:S(2)}) collective-permute-start(bf16[512,512]{1,0:T(8,128)(2,1)S(1)} %get-tuple-element.63), channel_id=1, source_target_pairs={{0,2},{1,3},{2,4},{3,5},{4,6},{5,7},{6,0},{7,1},{8,10},{9,11},{10,... | collective-permute-start | bytes 1572872 | tf_op jit(solution)/shard_map/ppermute | solution.py:220
  89.8 97.7 %collective-permute-start.24 = (bf16[2048,1024]{1,0:T(8,128)(2,1)}, bf16[2048,1024]{1,0:T(8,128)(2,1)}, u32[]{:S(2)}, u32[]{:S(2)}) collective-permute-start(bf16[2048,1024]{1,0:T(8,128)(2,1)} %param.12), channel_id=1, source_target_pairs={{0,8},{8,0},{16,24},{24,16},{1,9},{9,1},{17,25},{25,17},{2,10},{10... | collective-permute-start | bytes 12582920 | tf_op jit(solution)/shard_map/ppermute | solution.py:261
  113.3 26.2 %collective-permute-start.2 = (bf16[1024,512]{1,0:T(8,128)(2,1)S(1)}, bf16[1024,512]{1,0:T(8,128)(2,1)}, u32[]{:S(2)}, u32[]{:S(2)}) collective-permute-start(bf16[1024,512]{1,0:T(8,128)(2,1)S(1)} %collective-permute-done.1.refs_2_), channel_id=1, source_target_pairs={{0,1},{1,0},{2,3},{3,2},{4,5},{5,4},{6,7},{7,6},{8,9},{9,8},{10,11... | collective-permute-start | bytes 3145736 | tf_op jit(solution)/shard_map/ppermute | solution.py:229
  114.6 26.4 %collective-permute-start.10 = (bf16[512,512]{1,0:T(8,128)(2,1)}, bf16[512,512]{1,0:T(8,128)(2,1)}, u32[]{:S(2)}, u32[]{:S(2)}) collective-permute-start(bf16[512,512]{1,0:T(8,128)(2,1)} %collective-permute-done.6.refs_7_), channel_id=1, source_target_pairs={{0,2},{1,3},{2,4},{3,5},{4,6},{5,7},{6,0},{7,1},{8,10},{9,11},{10,... | collective-permute-start | bytes 1572872 | tf_op jit(solution)/shard_map/ppermute | solution.py:227
  116.3 34.0 %collective-permute-start.8 = (bf16[512,512]{1,0:T(8,128)(2,1)}, bf16[512,512]{1,0:T(8,128)(2,1)}, u32[]{:S(2)}, u32[]{:S(2)}) collective-permute-start(bf16[512,512]{1,0:T(8,128)(2,1)} %collective-permute-done.7.refs_8_), channel_id=1, source_target_pairs={{0,1},{1,0},{2,3},{3,2},{4,5},{5,4},{6,7},{7,6},{8,9},{9,8},{10,11... | collective-permute-start | bytes 1572872 | tf_op jit(solution)/shard_map/ppermute | solution.py:229
  139.5 31.6 %collective-permute-start.27 = (bf16[2048,128]{1,0:T(8,128)(2,1)}, bf16[2048,128]{1,0:T(8,128)(2,1)}, u32[]{:S(2)}, u32[]{:S(2)}) collective-permute-start(bf16[2048,128]{1,0:T(8,128)(2,1)} %get-tuple-element.34), channel_id=1, source_target_pairs={{0,16},{8,24},{16,0},{24,8},{1,17},{9,25},{17,1},{25,9},{2,18},{10... | collective-permute-start | bytes 1572872 | tf_op jit(solution)/shard_map/ppermute | solution.py:281
  141.0 31.7 %collective-permute-start.25 = (bf16[2048,128]{1,0:T(8,128)(2,1)}, bf16[2048,128]{1,0:T(8,128)(2,1)S(1)}, u32[]{:S(2)}, u32[]{:S(2)}) collective-permute-start(bf16[2048,128]{1,0:T(8,128)(2,1)} %get-tuple-element.29), channel_id=1, source_target_pairs={{0,16},{8,24},{16,0},{24,8},{1,17},{9,25},{17,1},{25,9},{2,18},{10... | collective-permute-start | bytes 1572872 | tf_op jit(solution)/shard_map/ppermute | solution.py:281
  150.3 94.5 %collective-permute-start.35 = (bf16[2048,256]{1,0:T(8,128)(2,1)}, bf16[2048,256]{1,0:T(8,128)(2,1)}, u32[]{:S(2)}, u32[]{:S(2)}) collective-permute-start(bf16[2048,256]{1,0:T(8,128)(2,1)} %pad_maximum_fusion), channel_id=1, source_target_pairs={{0,16},{8,24},{16,0},{24,8},{1,17},{9,25},{17,1},{25,9},{2,18},{10... | collective-permute-start | bytes 3145736 | tf_op jit(solution)/shard_map/ppermute | solution.py:281
  171.2 74.2 %collective-permute-start.43 = (bf16[2048,256]{1,0:T(8,128)(2,1)}, bf16[2048,256]{1,0:T(8,128)(2,1)}, u32[]{:S(2)}, u32[]{:S(2)}) collective-permute-start(bf16[2048,256]{1,0:T(8,128)(2,1)} %pad_maximum_fusion.1), channel_id=1, source_target_pairs={{0,16},{8,24},{16,0},{24,8},{1,17},{9,25},{17,1},{25,9},{2,18},{10... | collective-permute-start | bytes 3145736 | tf_op jit(solution)/shard_map/ppermute | solution.py:281
  172.7 48.0 %collective-permute-start.20 = (bf16[128,1536]{1,0:T(8,128)(2,1)}, bf16[128,1536]{1,0:T(8,128)(2,1)S(1)}, u32[]{:S(2)}, u32[]{:S(2)}) collective-permute-start(bf16[128,1536]{1,0:T(8,128)(2,1)} %get-tuple-element.19), channel_id=1, source_target_pairs={{0,8},{8,16},{16,24},{1,9},{9,17},{17,25},{2,10},{10,18},{18,26},{... | collective-permute-start | bytes 1179656 | tf_op jit(solution)/shard_map/ppermute | solution.py:256
  175.3 45.5 %collective-permute-start.22 = (bf16[128,1536]{1,0:T(8,128)(2,1)}, bf16[128,1536]{1,0:T(8,128)(2,1)S(1)}, u32[]{:S(2)}, u32[]{:S(2)}) collective-permute-start(bf16[128,1536]{1,0:T(8,128)(2,1)} %get-tuple-element.21), channel_id=1, source_target_pairs={{8,0},{16,8},{24,16},{9,1},{17,9},{25,17},{10,2},{18,10},{26,18},{... | collective-permute-start | bytes 1179656 | tf_op jit(solution)/shard_map/ppermute | solution.py:255
  192.2 24.5 %collective-permute-start.23 = (bf16[128,512]{1,0:T(8,128)(2,1)}, bf16[128,512]{1,0:T(8,128)(2,1)S(1)}, u32[]{:S(2)}, u32[]{:S(2)}) collective-permute-start(bf16[128,512]{1,0:T(8,128)(2,1)} %get-tuple-element.22), channel_id=1, source_target_pairs={{8,0},{16,8},{24,16},{9,1},{17,9},{25,17},{10,2},{18,10},{26,18},{... | collective-permute-start | bytes 393224 | tf_op jit(solution)/shard_map/ppermute | solution.py:255
  244.1 26.4 %collective-permute-start.54 = (bf16[2048,128]{1,0:T(8,128)(2,1)S(1)}, bf16[2048,128]{1,0:T(8,128)(2,1)S(1)}, u32[]{:S(2)}, u32[]{:S(2)}) collective-permute-start(bf16[2048,128]{1,0:T(8,128)(2,1)S(1)} %collective-permute-done.53), channel_id=1, source_target_pairs={{0,8},{8,0},{16,24},{24,16},{1,9},{9,1},{17,25},{25,17},{2,10},{10... | collective-permute-start | bytes 1572872 | tf_op jit(solution)/shard_map/ppermute | solution.py:282
  244.8 31.2 %collective-permute-start.52 = (bf16[2048,128]{1,0:T(8,128)(2,1)S(1)}, bf16[2048,128]{1,0:T(8,128)(2,1)S(1)}, u32[]{:S(2)}, u32[]{:S(2)}) collective-permute-start(bf16[2048,128]{1,0:T(8,128)(2,1)S(1)} %collective-permute-done.51), channel_id=1, source_target_pairs={{0,8},{8,0},{16,24},{24,16},{1,9},{9,1},{17,25},{25,17},{2,10},{10... | collective-permute-start | bytes 1572872 | tf_op jit(solution)/shard_map/ppermute | solution.py:282
  251.0 30.9 %collective-permute-start.29 = (bf16[512,512]{0,1:T(8,128)(2,1)S(1)}, bf16[512,512]{0,1:T(8,128)(2,1)S(1)}, u32[]{:S(2)}, u32[]{:S(2)}) collective-permute-start(bf16[512,512]{0,1:T(8,128)(2,1)S(1)} %pad_maximum_fusion.2), channel_id=1, source_target_pairs={{0,1},{1,0},{2,3},{3,2},{4,5},{5,4},{6,7},{7,6},{8,9},{9,8},{10,11... | collective-permute-start | bytes 1572872 | tf_op jit(solution)/shard_map/ppermute | solution.py:300
  259.5 65.2 %collective-permute-start.32 = (bf16[512,512]{0,1:T(8,128)(2,1)S(1)}, bf16[512,512]{0,1:T(8,128)(2,1)S(1)}, u32[]{:S(2)}, u32[]{:S(2)}) collective-permute-start(bf16[512,512]{0,1:T(8,128)(2,1)S(1)} %pad_maximum_fusion.5), channel_id=1, source_target_pairs={{0,2},{1,3},{2,0},{3,1},{4,6},{5,7},{6,4},{7,5},{8,10},{9,11},{10,... | collective-permute-start | bytes 1572872 | tf_op jit(solution)/shard_map/ppermute | solution.py:320
  281.9 29.3 %collective-permute-start.48 = (bf16[512,512]{0,1:T(8,128)(2,1)S(1)}, bf16[512,512]{0,1:T(8,128)(2,1)S(1)}, u32[]{:S(2)}, u32[]{:S(2)}) collective-permute-start(bf16[512,512]{0,1:T(8,128)(2,1)S(1)} %pad_maximum_fusion.9), channel_id=1, source_target_pairs={{0,1},{1,0},{2,3},{3,2},{4,5},{5,4},{6,7},{7,6},{8,9},{9,8},{10,11... | collective-permute-start | bytes 1572872 | tf_op jit(solution)/shard_map/ppermute | solution.py:300
  283.3 39.1 %collective-permute-start.55 = (bf16[512,512]{0,1:T(8,128)(2,1)S(1)}, bf16[512,512]{0,1:T(8,128)(2,1)S(1)}, u32[]{:S(2)}, u32[]{:S(2)}) collective-permute-start(bf16[512,512]{0,1:T(8,128)(2,1)S(1)} %pad_maximum_fusion.10), channel_id=1, source_target_pairs={{0,1},{1,0},{2,3},{3,2},{4,5},{5,4},{6,7},{7,6},{8,9},{9,8},{10,11... | collective-permute-start | bytes 1572872 | tf_op jit(solution)/shard_map/ppermute | solution.py:300
  288.7 44.1 %collective-permute-start.58 = (bf16[512,512]{0,1:T(8,128)(2,1)S(1)}, bf16[512,512]{0,1:T(8,128)(2,1)S(1)}, u32[]{:S(2)}, u32[]{:S(2)}) collective-permute-start(bf16[512,512]{0,1:T(8,128)(2,1)S(1)} %pad_maximum_fusion.11), channel_id=1, source_target_pairs={{0,1},{1,0},{2,3},{3,2},{4,5},{5,4},{6,7},{7,6},{8,9},{9,8},{10,11... | collective-permute-start | bytes 1572872 | tf_op jit(solution)/shard_map/ppermute | solution.py:300
  299.9 47.0 %collective-permute-start.30 = (bf16[512,256]{0,1:T(8,128)(2,1)S(1)}, bf16[512,256]{0,1:T(8,128)(2,1)S(1)}, u32[]{:S(2)}, u32[]{:S(2)}) collective-permute-start(bf16[512,256]{0,1:T(8,128)(2,1)S(1)} %pad_maximum_fusion.12), channel_id=1, source_target_pairs={{0,2},{1,3},{2,0},{3,1},{4,6},{5,7},{6,4},{7,5},{8,10},{9,11},{10,... | collective-permute-start | bytes 786440 | tf_op jit(solution)/shard_map/ppermute | solution.py:320
  311.2 37.9 %collective-permute-start.38 = (bf16[512,256]{0,1:T(8,128)(2,1)S(1)}, bf16[512,256]{0,1:T(8,128)(2,1)S(1)}, u32[]{:S(2)}, u32[]{:S(2)}) collective-permute-start(bf16[512,256]{0,1:T(8,128)(2,1)S(1)} %pad_maximum_fusion.13), channel_id=1, source_target_pairs={{0,2},{1,3},{2,0},{3,1},{4,6},{5,7},{6,4},{7,5},{8,10},{9,11},{10,... | collective-permute-start | bytes 786440 | tf_op jit(solution)/shard_map/ppermute | solution.py:320
  322.4 26.8 %collective-permute-start.41 = (bf16[512,256]{0,1:T(8,128)(2,1)S(1)}, bf16[512,256]{0,1:T(8,128)(2,1)S(1)}, u32[]{:S(2)}, u32[]{:S(2)}) collective-permute-start(bf16[512,256]{0,1:T(8,128)(2,1)S(1)} %pad_maximum_fusion.14), channel_id=1, source_target_pairs={{0,2},{1,3},{2,0},{3,1},{4,6},{5,7},{6,4},{7,5},{8,10},{9,11},{10,... | collective-permute-start | bytes 786440 | tf_op jit(solution)/shard_map/ppermute | solution.py:320
  324.7 26.4 %collective-permute-start.46 = (bf16[512,256]{0,1:T(8,128)(2,1)S(1)}, bf16[512,256]{0,1:T(8,128)(2,1)S(1)}, u32[]{:S(2)}, u32[]{:S(2)}) collective-permute-start(bf16[512,256]{0,1:T(8,128)(2,1)S(1)} %pad_maximum_fusion.15), channel_id=1, source_target_pairs={{0,2},{1,3},{2,0},{3,1},{4,6},{5,7},{6,4},{7,5},{8,10},{9,11},{10,... | collective-permute-start | bytes 786440 | tf_op jit(solution)/shard_map/ppermute | solution.py:320
  349.3 24.4 %collective-permute-start.31 = (bf16[512,128]{0,1:T(8,128)(2,1)S(1)}, bf16[512,128]{0,1:T(8,128)(2,1)S(1)}, u32[]{:S(2)}, u32[]{:S(2)}) collective-permute-start(bf16[512,128]{0,1:T(8,128)(2,1)S(1)} %add_convert_fusion.7), channel_id=1, source_target_pairs={{0,4},{1,5},{2,6},{3,7},{4,0},{5,1},{6,2},{7,3},{8,12},{9,13},{10,... | collective-permute-start | bytes 393224 | tf_op jit(solution)/shard_map/ppermute | solution.py:320
  360.3 24.1 %collective-permute-start.39 = (bf16[512,128]{0,1:T(8,128)(2,1)S(1)}, bf16[512,128]{0,1:T(8,128)(2,1)S(1)}, u32[]{:S(2)}, u32[]{:S(2)}) collective-permute-start(bf16[512,128]{0,1:T(8,128)(2,1)S(1)} %add_convert_fusion.6), channel_id=1, source_target_pairs={{0,4},{1,5},{2,6},{3,7},{4,0},{5,1},{6,2},{7,3},{8,12},{9,13},{10,... | collective-permute-start | bytes 393224 | tf_op jit(solution)/shard_map/ppermute | solution.py:320
  (50 other events, 981.8 us)

commit v3 on v2

--- a/solution.py
+++ b/solution.py
@@ -121,10 +121,15 @@
 
 def conv_kernel(parts, pre_ref, *refs):
     n = len(parts)
-    taps_ref, bias_ref, out_ref, left, right = refs[2 * n:]
+    taps_ref, bias_ref, out_ref, left, right, above, below = refs[2 * n:]
     for f, (lo, hi) in enumerate(parts):
-        inside = (pl.program_id(0) >= lo) & (pl.program_id(0) < hi)
-        pl.when(inside)(functools.partial(conv_tile, pre_ref, refs[f], refs[n + f], taps_ref, bias_ref, out_ref, left, right))
+
+        @pl.when((pl.program_id(0) >= lo) & (pl.program_id(0) < hi))
+        def _(f=f):
+            above[...] = refs[f][...]
+            below[...] = refs[n + f][...]
+
+    conv_tile(pre_ref, above, below, taps_ref, bias_ref, out_ref, left, right)
 
 
 def conv_tile(pre_ref, before_ref, after_ref, taps_ref, bias_ref, out_ref, left, right):
@@ -177,7 +182,7 @@
         in_specs=[wide(rows)] + edges + edges + [wide(9), wide(1)],
         out_specs=wide(rows),
         out_shape=jax.ShapeDtypeStruct((rows, hidden), jnp.bfloat16),
-        scratch_shapes=[pltpu.VMEM((GRIDW + 16, LANES), jnp.float32)] * 2,
+        scratch_shapes=[pltpu.VMEM((GRIDW + 16, LANES), jnp.float32)] * 2 + [pltpu.VMEM((BAND, tile), jnp.bfloat16)] * 2,
         compiler_params=pltpu.CompilerParams(vmem_limit_bytes=24 << 20),
         cost_estimate=pl.CostEstimate(flops=60 * rows * hidden, bytes_accessed=4 * rows * hidden, transcendentals=0),
     )(pre, *befores, *afters, taps, bias[None])
@@ -272,7 +277,7 @@
         theirs = cut_of(partner_out)
         near = [joint, jnp.concatenate([theirs[k] for k in order], axis=1)]
         near = [jnp.dot(act, b, preferred_element_type=jnp.float32).astype(jnp.bfloat16) for b in near]
-        apart = q in (0, pieces - 1)
+        apart = q == 0
         groups = [[k] for k in order] if apart else [order]
         far = {}
         for group in groups:

time: 409 us -> 416 us (1.017)
  waiting for transfers between devices: 246 us -> 256 us
  matrix products: 33.1 us -> 28.3 us
    ppermute x6 -> x5, waiting for transfers between devices: 7.1 us -> 41.3 us  [local(): mine = lax.ppermute(block, 'tok', yshift(j))]
    ppermute x2, waiting for transfers between devices: 23 us -> 0.01 us  [local(): afters.append(lax.ppermute(first, 'tok', down))]
    ppermute x1, waiting for transfers between devices: 19.4 us -> 0.01 us  [local(): held = [lax.ppermute(tokens, 'ch', zshift(1))]]
    ppermute x4, waiting for transfers between devices: 51.4 us -> 70.6 us  [local(): mine = lax.ppermute(w_in[:, n * tile:(n + 1) * tile], 'tok', yshift(k))]
    dot_general x20 -> x18, matrix products: 33.1 us -> 28.3 us  [local(): jnp.dot(act, b, preferred_element_type=jnp.float32).astype(jnp.bfloat16)]
    ppermute x16, waiting for transfers between devices: 55.9 us -> 51.3 us  [local(): lax.ppermute(packed, 'ch', [(i, (i // nx ^ bit) * nx + i % nx) for i in r...]
    ppermute x6 -> x5, starting transfers between devices: 9.22 us -> 5.64 us  [local(): mine = lax.ppermute(block, 'tok', yshift(j))]
  transfers between devices with their start and end apart: 61 -> 59, of which waited for: 30 -> 29; matrix products, arithmetic and copies ran while one was open for 12% -> 11% of each run, Pallas kernels for 10% -> 10%
where the time goes in v3:
time: 416 us; the launch traced here: 408 us
  waiting for transfers between devices  256 us (62%)
  starting transfers between devices  65.7 us (16%)
  Pallas kernels  39.5 us (9%)
  matrix products  28.3 us (7%)
  local copies, waits for them, and re-layouts  10.9 us (3%)
  other arithmetic  5.99 us (1%)
    ppermute x4, waiting for transfers between devices, local(): mine = lax.ppermute(w_in[:, n * tile:(n + 1) * tile], 'tok', yshift(k))  70.6 us
    ppermute x16, waiting for transfers between devices, local(): lax.ppermute(packed, 'ch', [(i, (i // nx ^ bit) * nx + i % nx) for i in r...  51.3 us
    ppermute x7, waiting for transfers between devices, local(): lax.ppermute(shares(k, cut), 'ch', xshift(k))  42.1 us
    ppermute x5, waiting for transfers between devices, local(): mine = lax.ppermute(block, 'tok', yshift(j))  41.3 us
    ppermute x5, waiting for transfers between devices, local(): got = lax.ppermute(block, 'ch', xshift(k))  35.8 us
    pallas_call x2, Pallas kernels, project(): pl.pallas_call(functools.partial(mm_kernel, places, homes, base), in_spec...  30.2 us
    dot_general x18, matrix products, local(): jnp.dot(act, b, preferred_element_type=jnp.float32).astype(jnp.bfloat16)  28.3 us
    ppermute x16, starting transfers between devices, local(): lax.ppermute(packed, 'ch', [(i, (i // nx ^ bit) * nx + i % nx) for i in r...  18 us
  transfers between devices with their start and end apart: 59, of which 29 were waited for; matrix products, arithmetic and copies ran while one was open for 11% of the time, Pallas kernels for 10%

profile of v3, /device:TPU:0, one launch (start us, length us, event | category | flops | bytes accessed | tf_op | source)
XLA Modules:
  0.0 408.0 jit_solution(15600736649042900389)
XLA Ops:
  0.0 3.1 collective-permute-start.1
  12.4 8.2 %collective-permute-done.27 = bf16[2048,128]{1,0:T(8,128)(2,1)S(1)} collective-permute-done((bf16[2048,128]{1,0:T(8,128)(2,1)S(1)}, bf16[2048,128]{1,0:T(8,128)(2,1)S(1)}, u32[]{:S(2)}, u32[]{:S(2)}) %collective-permute-start.27) | collective-permute-done | bytes 524320 | tf_op jit(solution)/shard_map/ppermute | solution.py:286
  22.0 9.7 %collective-permute-done.25 = bf16[2048,128]{1,0:T(8,128)(2,1)S(1)} collective-permute-done((bf16[2048,128]{1,0:T(8,128)(2,1)S(1)}, bf16[2048,128]{1,0:T(8,128)(2,1)S(1)}, u32[]{:S(2)}, u32[]{:S(2)}) %collective-permute-start.25) | collective-permute-done | bytes 524320 | tf_op jit(solution)/shard_map/ppermute | solution.py:286
  33.4 20.8 %collective-permute-done.14.refs_14_ = bf16[1024,512]{1,0:T(8,128)(2,1)S(1)} collective-permute-done((bf16[1024,512]{1,0:T(8,128)(2,1)S(1)}, bf16[1024,512]{1,0:T(8,128)(2,1)S(1)}, u32[]{:S(2)}, u32[]{:S(2)}) %collective-permute-start.14) | collective-permute-done | bytes 1048608 | tf_op jit(solution)/shard_map/ppermute | solution.py:247
  55.8 20.9 %collective-permute-done.16.refs_16_ = bf16[1024,512]{1,0:T(8,128)(2,1)S(1)} collective-permute-done((bf16[1024,512]{1,0:T(8,128)(2,1)S(1)}, bf16[1024,512]{1,0:T(8,128)(2,1)S(1)}, u32[]{:S(2)}, u32[]{:S(2)}) %collective-permute-start.16) | collective-permute-done | bytes 1048608 | tf_op jit(solution)/shard_map/ppermute | solution.py:247
  78.3 20.9 %collective-permute-done.18.refs_18_ = bf16[1024,512]{1,0:T(8,128)(2,1)S(1)} collective-permute-done((bf16[1024,512]{1,0:T(8,128)(2,1)S(1)}, bf16[1024,512]{1,0:T(8,128)(2,1)S(1)}, u32[]{:S(2)}, u32[]{:S(2)}) %collective-permute-start.18) | collective-permute-done | bytes 1048608 | tf_op jit(solution)/shard_map/ppermute | solution.py:247
  102.2 9.8 %collective-permute-done.3.refs_4_ = bf16[512,512]{1,0:T(8,128)(2,1)S(1)} collective-permute-done((bf16[512,512]{1,0:T(8,128)(2,1)S(1)}, bf16[512,512]{1,0:T(8,128)(2,1)S(1)}, u32[]{:S(2)}, u32[]{:S(2)}) %collective-permute-start.3) | collective-permute-done | bytes 524320 | tf_op jit(solution)/shard_map/ppermute | solution.py:225
  112.3 8.0 %collective-permute-done.12.refs_14_ = bf16[1024,512]{1,0:T(8,128)(2,1)} collective-permute-done((bf16[1024,512]{1,0:T(8,128)(2,1)S(1)}, bf16[1024,512]{1,0:T(8,128)(2,1)}, u32[]{:S(2)}, u32[]{:S(2)}) %collective-permute-start.12) | collective-permute-done | bytes 1048608 | tf_op jit(solution)/shard_map/ppermute | solution.py:247
  124.3 8.6 %collective-permute-done.4.refs_5_ = bf16[512,512]{1,0:T(8,128)(2,1)S(1)} collective-permute-done((bf16[512,512]{1,0:T(8,128)(2,1)S(1)}, bf16[512,512]{1,0:T(8,128)(2,1)S(1)}, u32[]{:S(2)}, u32[]{:S(2)}) %collective-permute-start.4) | collective-permute-done | bytes 524320 | tf_op jit(solution)/shard_map/ppermute | solution.py:234
  132.9 3.0 collective-permute-done.9.refs_10_
  143.6 18.5 %collective-permute-done.2.refs_3_ = bf16[1024,512]{1,0:T(8,128)(2,1)} collective-permute-done((bf16[1024,512]{1,0:T(8,128)(2,1)S(1)}, bf16[1024,512]{1,0:T(8,128)(2,1)}, u32[]{:S(2)}, u32[]{:S(2)}) %collective-permute-start.2) | collective-permute-done | bytes 1048608 | tf_op jit(solution)/shard_map/ppermute | solution.py:234
  164.2 8.7 %collective-permute-done.8.refs_9_ = bf16[512,512]{1,0:T(8,128)(2,1)} collective-permute-done((bf16[512,512]{1,0:T(8,128)(2,1)}, bf16[512,512]{1,0:T(8,128)(2,1)}, u32[]{:S(2)}, u32[]{:S(2)}) %collective-permute-start.8) | collective-permute-done | bytes 524320 | tf_op jit(solution)/shard_map/ppermute | solution.py:234
  174.4 19.4 %shard_map.73 = (bf16[1024,2048]{1,0:T(8,128)(2,1)}, bf16[128,1536]{1,0:T(8,128)(2,1)}, bf16[128,1536]{1,0:T(8,128)(2,1)}) custom-call(s32[6]{0:T(128)} %stack.27.start_ref, f32[1,2048]{1,0:T(1,128)} %bitcast.37, bf16[1024,512]{1,0:T(8,128)(2,1)} %refs_0_.3, bf16[1024,512]{1,0:T(8,128)(2,1)} %copy-done.9, bf16[1024,512]{1,0:T(8,128)(2,1)} %copy-done.3, ...), custom_call_target="tpu_custom_call" | custom-call | flops 12884901888 | bytes 20971520 | tf_op jit(solution)/shard_map/pallas_call | solution.py:101
  193.8 3.1 collective-permute-start.20
  198.2 10.8 %shard_map.74 = (bf16[1024,2048]{1,0:T(8,128)(2,1)}, bf16[128,512]{1,0:T(8,128)(2,1)}, bf16[128,512]{1,0:T(8,128)(2,1)}) custom-call(s32[6]{0:T(128)} %stack.27.start_ref, f32[1,2048]{1,0:T(1,128)} %bitcast.38, bf16[1024,512]{1,0:T(8,128)(2,1)} %refs_0_.3, bf16[1024,512]{1,0:T(8,128)(2,1)} %copy-done.9, ...), custom_call_target="tpu_custom_call", output_to_operand_aliasing={{0}: (18, {})} | custom-call | flops 4294967296 | bytes 12582912 | tf_op jit(solution)/shard_map/pallas_call | solution.py:101
  210.9 21.5 %collective-permute-done.51 = bf16[2048,256]{1,0:T(8,128)(2,1)} collective-permute-done((bf16[2048,256]{1,0:T(8,128)(2,1)}, bf16[2048,256]{1,0:T(8,128)(2,1)}, u32[]{:S(2)}, u32[]{:S(2)}) %collective-permute-start.51) | collective-permute-done | bytes 1048608 | tf_op jit(solution)/shard_map/ppermute | solution.py:286
  238.0 3.9 collective-permute-start.26
  244.3 9.3 %shard_map.75 = bf16[1024,2048]{1,0:T(8,128)(2,1)S(1)} custom-call(bf16[1024,2048]{1,0:T(8,128)(2,1)S(1)} %copy-done, bf16[128,1536]{1,0:T(8,128)(2,1)S(1)} %collective-permute-done.20.refs_0_, bf16[128,512]{1,0:T(8,128)(2,1)S(1)} %collective-permute-done.21.refs_1_, bf16[128,1536]{1,0:T(8,128)(2,1)S(1)} %collective-permute-done.22.refs_2_, ...), custom_call_target="tpu_custom_call" | custom-call | flops 125829120 | bytes 8388608 | tf_op jit(solution)/shard_map/pallas_call | solution.py:179
  290.6 6.5 %collective-permute-done.40 = bf16[512,512]{0,1:T(8,128)(2,1)S(1)} collective-permute-done((bf16[512,512]{0,1:T(8,128)(2,1)S(1)}, bf16[512,512]{0,1:T(8,128)(2,1)S(1)}, u32[]{:S(2)}, u32[]{:S(2)}) %collective-permute-start.40) | collective-permute-done | bytes 524320 | tf_op jit(solution)/shard_map/ppermute | solution.py:305
  298.4 10.0 %collective-permute-done.45 = bf16[512,512]{0,1:T(8,128)(2,1)S(1)} collective-permute-done((bf16[512,512]{0,1:T(8,128)(2,1)S(1)}, bf16[512,512]{0,1:T(8,128)(2,1)S(1)}, u32[]{:S(2)}, u32[]{:S(2)}) %collective-permute-start.45) | collective-permute-done | bytes 524320 | tf_op jit(solution)/shard_map/ppermute | solution.py:305
  310.6 9.0 %collective-permute-done.48 = bf16[512,512]{0,1:T(8,128)(2,1)S(1)} collective-permute-done((bf16[512,512]{0,1:T(8,128)(2,1)S(1)}, bf16[512,512]{0,1:T(8,128)(2,1)S(1)}, u32[]{:S(2)}, u32[]{:S(2)}) %collective-permute-start.48) | collective-permute-done | bytes 524320 | tf_op jit(solution)/shard_map/ppermute | solution.py:305
  322.0 8.8 %collective-permute-done.53 = bf16[512,512]{0,1:T(8,128)(2,1)S(1)} collective-permute-done((bf16[512,512]{0,1:T(8,128)(2,1)S(1)}, bf16[512,512]{0,1:T(8,128)(2,1)S(1)}, u32[]{:S(2)}, u32[]{:S(2)}) %collective-permute-start.53) | collective-permute-done | bytes 524320 | tf_op jit(solution)/shard_map/ppermute | solution.py:305
  333.3 7.7 %collective-permute-done.56 = bf16[512,512]{0,1:T(8,128)(2,1)S(1)} collective-permute-done((bf16[512,512]{0,1:T(8,128)(2,1)S(1)}, bf16[512,512]{0,1:T(8,128)(2,1)S(1)}, u32[]{:S(2)}, u32[]{:S(2)}) %collective-permute-start.56) | collective-permute-done | bytes 524320 | tf_op jit(solution)/shard_map/ppermute | solution.py:305
  342.0 12.7 %collective-permute-done.33 = bf16[512,256]{0,1:T(8,128)(2,1)S(1)} collective-permute-done((bf16[512,256]{0,1:T(8,128)(2,1)S(1)}, bf16[512,256]{0,1:T(8,128)(2,1)S(1)}, u32[]{:S(2)}, u32[]{:S(2)}) %collective-permute-start.33) | collective-permute-done | bytes 262176 | tf_op jit(solution)/shard_map/ppermute | solution.py:325
  360.3 6.3 %collective-permute-done.49 = bf16[512,256]{0,1:T(8,128)(2,1)S(1)} collective-permute-done((bf16[512,256]{0,1:T(8,128)(2,1)S(1)}, bf16[512,256]{0,1:T(8,128)(2,1)S(1)}, u32[]{:S(2)}, u32[]{:S(2)}) %collective-permute-start.49) | collective-permute-done | bytes 262176 | tf_op jit(solution)/shard_map/ppermute | solution.py:325
  367.5 8.0 %collective-permute-done.54 = bf16[512,256]{0,1:T(8,128)(2,1)S(1)} collective-permute-done((bf16[512,256]{0,1:T(8,128)(2,1)S(1)}, bf16[512,256]{0,1:T(8,128)(2,1)S(1)}, u32[]{:S(2)}, u32[]{:S(2)}) %collective-permute-start.54) | collective-permute-done | bytes 262176 | tf_op jit(solution)/shard_map/ppermute | solution.py:325
  375.5 3.8 collective-permute-done.57
  379.4 3.0 collective-permute-start.50
  382.6 3.0 collective-permute-start.58
  385.6 8.4 %collective-permute-done.42 = bf16[512,128]{0,1:T(8,128)(2,1)S(1)} collective-permute-done((bf16[512,128]{0,1:T(8,128)(2,1)S(1)}, bf16[512,128]{0,1:T(8,128)(2,1)S(1)}, u32[]{:S(2)}, u32[]{:S(2)}) %collective-permute-start.42) | collective-permute-done | bytes 131104 | tf_op jit(solution)/shard_map/ppermute | solution.py:325
  396.9 4.2 %collective-permute-done.50 = bf16[512,128]{0,1:T(8,128)(2,1)S(1)} collective-permute-done((bf16[512,128]{0,1:T(8,128)(2,1)S(1)}, bf16[512,128]{0,1:T(8,128)(2,1)S(1)}, u32[]{:S(2)}, u32[]{:S(2)}) %collective-permute-start.50) | collective-permute-done | bytes 131104 | tf_op jit(solution)/shard_map/ppermute | solution.py:325
  401.1 2.8 collective-permute-done.55
  (242 shorter events, 104.2 us)
Async XLA Ops:
  0.0 31.8 %collective-permute-start.1 = (bf16[1024,512]{1,0:T(8,128)(2,1)}, bf16[1024,512]{1,0:T(8,128)(2,1)S(1)}, u32[]{:S(2)}, u32[]{:S(2)}) collective-permute-start(bf16[1024,512]{1,0:T(8,128)(2,1)} %refs_0_.3), channel_id=1, source_target_pairs={{0,2},{1,3},{2,4},{3,5},{4,6},{5,7},{6,0},{7,1},{8,10},{9,11},{10,... | collective-permute-start | bytes 3145736 | tf_op jit(solution)/shard_map/ppermute | solution.py:222
  7.3 24.5 %collective-permute-start.25 = (bf16[2048,128]{1,0:T(8,128)(2,1)S(1)}, bf16[2048,128]{1,0:T(8,128)(2,1)S(1)}, u32[]{:S(2)}, u32[]{:S(2)}) collective-permute-start(bf16[2048,128]{1,0:T(8,128)(2,1)S(1)} %get-tuple-element.29), channel_id=1, source_target_pairs={{0,16},{8,24},{16,0},{24,8},{1,17},{9,25},{17,1},{25,9},{2,18},{10... | collective-permute-start | bytes 1572872 | tf_op jit(solution)/shard_map/ppermute | solution.py:286
  10.3 44.0 %collective-permute-start.14 = (bf16[1024,512]{1,0:T(8,128)(2,1)S(1)}, bf16[1024,512]{1,0:T(8,128)(2,1)S(1)}, u32[]{:S(2)}, u32[]{:S(2)}) collective-permute-start(bf16[1024,512]{1,0:T(8,128)(2,1)S(1)} %get-tuple-element.47), channel_id=1, source_target_pairs={{0,16},{8,24},{16,0},{24,8},{1,17},{9,25},{17,1},{25,9},{2,18},{10... | collective-permute-start | bytes 3145736 | tf_op jit(solution)/shard_map/ppermute | solution.py:247
  11.8 64.9 %collective-permute-start.16 = (bf16[1024,512]{1,0:T(8,128)(2,1)S(1)}, bf16[1024,512]{1,0:T(8,128)(2,1)S(1)}, u32[]{:S(2)}, u32[]{:S(2)}) collective-permute-start(bf16[1024,512]{1,0:T(8,128)(2,1)S(1)} %get-tuple-element.46), channel_id=1, source_target_pairs={{0,16},{8,24},{16,0},{24,8},{1,17},{9,25},{17,1},{25,9},{2,18},{10... | collective-permute-start | bytes 3145736 | tf_op jit(solution)/shard_map/ppermute | solution.py:247
  20.5 78.6 %collective-permute-start.18 = (bf16[1024,512]{1,0:T(8,128)(2,1)S(1)}, bf16[1024,512]{1,0:T(8,128)(2,1)S(1)}, u32[]{:S(2)}, u32[]{:S(2)}) collective-permute-start(bf16[1024,512]{1,0:T(8,128)(2,1)S(1)} %get-tuple-element.45), channel_id=1, source_target_pairs={{0,16},{8,24},{16,0},{24,8},{1,17},{9,25},{17,1},{25,9},{2,18},{10... | collective-permute-start | bytes 3145736 | tf_op jit(solution)/shard_map/ppermute | solution.py:247
  31.8 142.6 %collective-permute-start.11 = (bf16[1024,2048]{1,0:T(8,128)(2,1)}, bf16[1024,2048]{1,0:T(8,128)(2,1)}, u32[]{:S(2)}, u32[]{:S(2)}) collective-permute-start(bf16[1024,2048]{1,0:T(8,128)(2,1)} %refs_12_.3), channel_id=1, source_target_pairs={{0,8},{8,0},{16,24},{24,16},{1,9},{9,1},{17,25},{25,17},{2,10},{10... | collective-permute-start | bytes 12582920 | tf_op jit(solution)/shard_map/ppermute | solution.py:242
  31.8 80.5 %collective-permute-start = (bf16[1024,512]{1,0:T(8,128)(2,1)S(1)}, bf16[1024,512]{1,0:T(8,128)(2,1)S(1)}, u32[]{:S(2)}, u32[]{:S(2)}) collective-permute-start(bf16[1024,512]{1,0:T(8,128)(2,1)S(1)} %copy-done.8), channel_id=1, source_target_pairs={{0,1},{1,0},{2,3},{3,2},{4,5},{5,4},{6,7},{7,6},{8,9},{9,8},{10,11... | collective-permute-start | bytes 3145736 | tf_op jit(solution)/shard_map/ppermute | solution.py:234
  54.2 66.1 %collective-permute-start.12 = (bf16[1024,512]{1,0:T(8,128)(2,1)S(1)}, bf16[1024,512]{1,0:T(8,128)(2,1)}, u32[]{:S(2)}, u32[]{:S(2)}) collective-permute-start(bf16[1024,512]{1,0:T(8,128)(2,1)S(1)} %get-tuple-element.48), channel_id=1, source_target_pairs={{0,16},{8,24},{16,0},{24,8},{1,17},{9,25},{17,1},{25,9},{2,18},{10... | collective-permute-start | bytes 3145736 | tf_op jit(solution)/shard_map/ppermute | solution.py:247
  76.7 24.1 %collective-permute-start.5 = (bf16[512,512]{1,0:T(8,128)(2,1)S(1)}, bf16[512,512]{1,0:T(8,128)(2,1)S(1)}, u32[]{:S(2)}, u32[]{:S(2)}) collective-permute-start(bf16[512,512]{1,0:T(8,128)(2,1)S(1)} %get-tuple-element.63), channel_id=1, source_target_pairs={{0,2},{1,3},{2,4},{3,5},{4,6},{5,7},{6,0},{7,1},{8,10},{9,11},{10,... | collective-permute-start | bytes 1572872 | tf_op jit(solution)/shard_map/ppermute | solution.py:225
  112.3 121.4 %collective-permute-start.24 = (bf16[2048,1024]{1,0:T(8,128)(2,1)}, bf16[2048,1024]{1,0:T(8,128)(2,1)}, u32[]{:S(2)}, u32[]{:S(2)}) collective-permute-start(bf16[2048,1024]{1,0:T(8,128)(2,1)} %param.12), channel_id=1, source_target_pairs={{0,8},{8,0},{16,24},{24,16},{1,9},{9,1},{17,25},{25,17},{2,10},{10... | collective-permute-start | bytes 12582920 | tf_op jit(solution)/shard_map/ppermute | solution.py:266
  135.9 26.2 %collective-permute-start.2 = (bf16[1024,512]{1,0:T(8,128)(2,1)S(1)}, bf16[1024,512]{1,0:T(8,128)(2,1)}, u32[]{:S(2)}, u32[]{:S(2)}) collective-permute-start(bf16[1024,512]{1,0:T(8,128)(2,1)S(1)} %collective-permute-done.1.refs_2_), channel_id=1, source_target_pairs={{0,1},{1,0},{2,3},{3,2},{4,5},{5,4},{6,7},{7,6},{8,9},{9,8},{10,11... | collective-permute-start | bytes 3145736 | tf_op jit(solution)/shard_map/ppermute | solution.py:234
  137.0 26.6 %collective-permute-start.10 = (bf16[512,512]{1,0:T(8,128)(2,1)}, bf16[512,512]{1,0:T(8,128)(2,1)}, u32[]{:S(2)}, u32[]{:S(2)}) collective-permute-start(bf16[512,512]{1,0:T(8,128)(2,1)} %collective-permute-done.6.refs_7_), channel_id=1, source_target_pairs={{0,2},{1,3},{2,4},{3,5},{4,6},{5,7},{6,0},{7,1},{8,10},{9,11},{10,... | collective-permute-start | bytes 1572872 | tf_op jit(solution)/shard_map/ppermute | solution.py:232
  138.5 34.3 %collective-permute-start.8 = (bf16[512,512]{1,0:T(8,128)(2,1)}, bf16[512,512]{1,0:T(8,128)(2,1)}, u32[]{:S(2)}, u32[]{:S(2)}) collective-permute-start(bf16[512,512]{1,0:T(8,128)(2,1)} %collective-permute-done.7.refs_8_), channel_id=1, source_target_pairs={{0,1},{1,0},{2,3},{3,2},{4,5},{5,4},{6,7},{7,6},{8,9},{9,8},{10,11... | collective-permute-start | bytes 1572872 | tf_op jit(solution)/shard_map/ppermute | solution.py:234
  162.1 31.7 %collective-permute-start.35 = (bf16[2048,256]{1,0:T(8,128)(2,1)}, bf16[2048,256]{1,0:T(8,128)(2,1)}, u32[]{:S(2)}, u32[]{:S(2)}) collective-permute-start(bf16[2048,256]{1,0:T(8,128)(2,1)} %pad_maximum_fusion), channel_id=1, source_target_pairs={{0,16},{8,24},{16,0},{24,8},{1,17},{9,25},{17,1},{25,9},{2,18},{10... | collective-permute-start | bytes 3145736 | tf_op jit(solution)/shard_map/ppermute | solution.py:286
  163.6 47.3 %collective-permute-start.43 = (bf16[2048,256]{1,0:T(8,128)(2,1)}, bf16[2048,256]{1,0:T(8,128)(2,1)}, u32[]{:S(2)}, u32[]{:S(2)}) collective-permute-start(bf16[2048,256]{1,0:T(8,128)(2,1)} %pad_maximum_fusion.1), channel_id=1, source_target_pairs={{0,16},{8,24},{16,0},{24,8},{1,17},{9,25},{17,1},{25,9},{2,18},{10... | collective-permute-start | bytes 3145736 | tf_op jit(solution)/shard_map/ppermute | solution.py:286
  172.9 59.6 %collective-permute-start.51 = (bf16[2048,256]{1,0:T(8,128)(2,1)}, bf16[2048,256]{1,0:T(8,128)(2,1)}, u32[]{:S(2)}, u32[]{:S(2)}) collective-permute-start(bf16[2048,256]{1,0:T(8,128)(2,1)} %pad_maximum_fusion.2), channel_id=1, source_target_pairs={{0,16},{8,24},{16,0},{24,8},{1,17},{9,25},{17,1},{25,9},{2,18},{10... | collective-permute-start | bytes 3145736 | tf_op jit(solution)/shard_map/ppermute | solution.py:286
  193.8 50.0 %collective-permute-start.20 = (bf16[128,1536]{1,0:T(8,128)(2,1)}, bf16[128,1536]{1,0:T(8,128)(2,1)S(1)}, u32[]{:S(2)}, u32[]{:S(2)}) collective-permute-start(bf16[128,1536]{1,0:T(8,128)(2,1)} %get-tuple-element.19), channel_id=1, source_target_pairs={{0,8},{8,16},{16,24},{1,9},{9,17},{17,25},{2,10},{10,18},{18,26},{... | collective-permute-start | bytes 1179656 | tf_op jit(solution)/shard_map/ppermute | solution.py:261
  196.9 46.9 %collective-permute-start.22 = (bf16[128,1536]{1,0:T(8,128)(2,1)}, bf16[128,1536]{1,0:T(8,128)(2,1)S(1)}, u32[]{:S(2)}, u32[]{:S(2)}) collective-permute-start(bf16[128,1536]{1,0:T(8,128)(2,1)} %get-tuple-element.21), channel_id=1, source_target_pairs={{8,0},{16,8},{24,16},{9,1},{17,9},{25,17},{10,2},{18,10},{26,18},{... | collective-permute-start | bytes 1179656 | tf_op jit(solution)/shard_map/ppermute | solution.py:260
  210.9 44.0 %collective-permute-start.28 = (bf16[2048,128]{1,0:T(8,128)(2,1)}, bf16[2048,128]{1,0:T(8,128)(2,1)S(1)}, u32[]{:S(2)}, u32[]{:S(2)}) collective-permute-start(bf16[2048,128]{1,0:T(8,128)(2,1)} %copy-done.13), channel_id=1, source_target_pairs={{0,8},{8,0},{16,24},{24,16},{1,9},{9,1},{17,25},{25,17},{2,10},{10... | collective-permute-start | bytes 1572872 | tf_op jit(solution)/shard_map/ppermute | solution.py:287
  243.8 29.7 %collective-permute-start.44 = (bf16[2048,256]{1,0:T(8,128)(2,1)}, bf16[2048,256]{1,0:T(8,128)(2,1)S(1)}, u32[]{:S(2)}, u32[]{:S(2)}) collective-permute-start(bf16[2048,256]{1,0:T(8,128)(2,1)} %collective-permute-done.43), channel_id=1, source_target_pairs={{0,8},{8,0},{16,24},{24,16},{1,9},{9,1},{17,25},{25,17},{2,10},{10... | collective-permute-start | bytes 3145736 | tf_op jit(solution)/shard_map/ppermute | solution.py:287
  243.8 40.2 %collective-permute-start.52 = (bf16[2048,256]{1,0:T(8,128)(2,1)}, bf16[2048,256]{1,0:T(8,128)(2,1)S(1)}, u32[]{:S(2)}, u32[]{:S(2)}) collective-permute-start(bf16[2048,256]{1,0:T(8,128)(2,1)} %collective-permute-done.51), channel_id=1, source_target_pairs={{0,8},{8,0},{16,24},{24,16},{1,9},{9,1},{17,25},{25,17},{2,10},{10... | collective-permute-start | bytes 3145736 | tf_op jit(solution)/shard_map/ppermute | solution.py:287
  259.6 28.4 %collective-permute-start.29 = (bf16[512,512]{0,1:T(8,128)(2,1)S(1)}, bf16[512,512]{0,1:T(8,128)(2,1)S(1)}, u32[]{:S(2)}, u32[]{:S(2)}) collective-permute-start(bf16[512,512]{0,1:T(8,128)(2,1)S(1)} %pad_maximum_fusion.3), channel_id=1, source_target_pairs={{0,1},{1,0},{2,3},{3,2},{4,5},{5,4},{6,7},{7,6},{8,9},{9,8},{10,11... | collective-permute-start | bytes 1572872 | tf_op jit(solution)/shard_map/ppermute | solution.py:305
  264.0 69.1 %collective-permute-start.32 = (bf16[512,512]{0,1:T(8,128)(2,1)S(1)}, bf16[512,512]{0,1:T(8,128)(2,1)S(1)}, u32[]{:S(2)}, u32[]{:S(2)}) collective-permute-start(bf16[512,512]{0,1:T(8,128)(2,1)S(1)} %pad_maximum_fusion.6), channel_id=1, source_target_pairs={{0,2},{1,3},{2,0},{3,1},{4,6},{5,7},{6,4},{7,5},{8,10},{9,11},{10,... | collective-permute-start | bytes 1572872 | tf_op jit(solution)/shard_map/ppermute | solution.py:325
  283.9 24.4 %collective-permute-start.45 = (bf16[512,512]{0,1:T(8,128)(2,1)S(1)}, bf16[512,512]{0,1:T(8,128)(2,1)S(1)}, u32[]{:S(2)}, u32[]{:S(2)}) collective-permute-start(bf16[512,512]{0,1:T(8,128)(2,1)S(1)} %pad_maximum_fusion.9), channel_id=1, source_target_pairs={{0,1},{1,0},{2,3},{3,2},{4,5},{5,4},{6,7},{7,6},{8,9},{9,8},{10,11... | collective-permute-start | bytes 1572872 | tf_op jit(solution)/shard_map/ppermute | solution.py:305
  288.0 31.6 %collective-permute-start.48 = (bf16[512,512]{0,1:T(8,128)(2,1)S(1)}, bf16[512,512]{0,1:T(8,128)(2,1)S(1)}, u32[]{:S(2)}, u32[]{:S(2)}) collective-permute-start(bf16[512,512]{0,1:T(8,128)(2,1)S(1)} %pad_maximum_fusion.10), channel_id=1, source_target_pairs={{0,1},{1,0},{2,3},{3,2},{4,5},{5,4},{6,7},{7,6},{8,9},{9,8},{10,11... | collective-permute-start | bytes 1572872 | tf_op jit(solution)/shard_map/ppermute | solution.py:305
  289.3 41.6 %collective-permute-start.53 = (bf16[512,512]{0,1:T(8,128)(2,1)S(1)}, bf16[512,512]{0,1:T(8,128)(2,1)S(1)}, u32[]{:S(2)}, u32[]{:S(2)}) collective-permute-start(bf16[512,512]{0,1:T(8,128)(2,1)S(1)} %pad_maximum_fusion.11), channel_id=1, source_target_pairs={{0,1},{1,0},{2,3},{3,2},{4,5},{5,4},{6,7},{7,6},{8,9},{9,8},{10,11... | collective-permute-start | bytes 1572872 | tf_op jit(solution)/shard_map/ppermute | solution.py:305
  297.1 43.8 %collective-permute-start.56 = (bf16[512,512]{0,1:T(8,128)(2,1)S(1)}, bf16[512,512]{0,1:T(8,128)(2,1)S(1)}, u32[]{:S(2)}, u32[]{:S(2)}) collective-permute-start(bf16[512,512]{0,1:T(8,128)(2,1)S(1)} %pad_maximum_fusion.12), channel_id=1, source_target_pairs={{0,1},{1,0},{2,3},{3,2},{4,5},{5,4},{6,7},{7,6},{8,9},{9,8},{10,11... | collective-permute-start | bytes 1572872 | tf_op jit(solution)/shard_map/ppermute | solution.py:305
  308.4 46.4 %collective-permute-start.30 = (bf16[512,256]{0,1:T(8,128)(2,1)S(1)}, bf16[512,256]{0,1:T(8,128)(2,1)S(1)}, u32[]{:S(2)}, u32[]{:S(2)}) collective-permute-start(bf16[512,256]{0,1:T(8,128)(2,1)S(1)} %pad_maximum_fusion.13), channel_id=1, source_target_pairs={{0,2},{1,3},{2,0},{3,1},{4,6},{5,7},{6,4},{7,5},{8,10},{9,11},{10,... | collective-permute-start | bytes 786440 | tf_op jit(solution)/shard_map/ppermute | solution.py:325
  319.6 37.3 %collective-permute-start.38 = (bf16[512,256]{0,1:T(8,128)(2,1)S(1)}, bf16[512,256]{0,1:T(8,128)(2,1)S(1)}, u32[]{:S(2)}, u32[]{:S(2)}) collective-permute-start(bf16[512,256]{0,1:T(8,128)(2,1)S(1)} %pad_maximum_fusion.14), channel_id=1, source_target_pairs={{0,2},{1,3},{2,0},{3,1},{4,6},{5,7},{6,4},{7,5},{8,10},{9,11},{10,... | collective-permute-start | bytes 786440 | tf_op jit(solution)/shard_map/ppermute | solution.py:325
  330.8 26.2 %collective-permute-start.41 = (bf16[512,256]{0,1:T(8,128)(2,1)S(1)}, bf16[512,256]{0,1:T(8,128)(2,1)S(1)}, u32[]{:S(2)}, u32[]{:S(2)}) collective-permute-start(bf16[512,256]{0,1:T(8,128)(2,1)S(1)} %pad_maximum_fusion.15), channel_id=1, source_target_pairs={{0,2},{1,3},{2,0},{3,1},{4,6},{5,7},{6,4},{7,5},{8,10},{9,11},{10,... | collective-permute-start | bytes 786440 | tf_op jit(solution)/shard_map/ppermute | solution.py:325
  333.1 26.0 %collective-permute-start.46 = (bf16[512,256]{0,1:T(8,128)(2,1)S(1)}, bf16[512,256]{0,1:T(8,128)(2,1)S(1)}, u32[]{:S(2)}, u32[]{:S(2)}) collective-permute-start(bf16[512,256]{0,1:T(8,128)(2,1)S(1)} %pad_maximum_fusion.16), channel_id=1, source_target_pairs={{0,2},{1,3},{2,0},{3,1},{4,6},{5,7},{6,4},{7,5},{8,10},{9,11},{10,... | collective-permute-start | bytes 786440 | tf_op jit(solution)/shard_map/ppermute | solution.py:325
  357.0 25.4 %collective-permute-start.31 = (bf16[512,128]{0,1:T(8,128)(2,1)S(1)}, bf16[512,128]{0,1:T(8,128)(2,1)S(1)}, u32[]{:S(2)}, u32[]{:S(2)}) collective-permute-start(bf16[512,128]{0,1:T(8,128)(2,1)S(1)} %add_convert_fusion.7), channel_id=1, source_target_pairs={{0,4},{1,5},{2,6},{3,7},{4,0},{5,1},{6,2},{7,3},{8,12},{9,13},{10,... | collective-permute-start | bytes 393224 | tf_op jit(solution)/shard_map/ppermute | solution.py:325
  (57 other events, 1470.0 us)
